TPU v7x, 512 devices: a whole 4x4x16 slice. The times are simulated.
512 devices in a mesh: orb: 32 (over z, core), vec: 16 (over y, x).
Axes of the slice: x: 4, y: 4, z: 16, core: 2. Of those that a mesh axis runs over, the one named last changes fastest.
Arguments:
- orbitals: bfloat16 [32, 96, 9216], P('orb'), may hold values from -6 to 6
- energies: float32 [32], P('orb'), may hold values from -1 to 0
- trial_potential: bfloat16 [16, 96, 9216], P('vec', 'orb'), may hold values from -6 to 6
- local_potential: bfloat16 [96, 9216], P('orb'), may hold values from 0.5 to 2
Outputs:
- ortho: float32 [16, 96, 9216], P('vec', 'orb')
- factor: float32 [16, 16], replicated
All inputs are finite; a program needn't handle non-finite values.
Results may differ from a plain program's by a relative error of at most 0.0003.
Values may be sent and summed in bfloat16 or wider, within the bound.
A program may use at most 64 MiB of HBM per device.

v0:
```python
import jax
import jax.numpy as jnp
from jax import lax
from jax.sharding import Mesh
from jax.sharding import PartitionSpec as P

NZ = 96
NY = 96
NX = 96
STEPS = 4
ORB = ("orb_0", "orb_1")


def in_one_piece(arrays, axis, dim, along):
    ends, at = ([], 0)
    for a in arrays[:-1]:
        at += a.shape[along]
        ends.append(at)
    both = jnp.concatenate(arrays, axis=along)
    return tuple(jnp.split(lax.all_gather(both, axis, axis=dim, tiled=True), ends, axis=along))


def reduced_to_own(blocks, axes, order):
    shape = [lax.axis_size(a) for a in axes]
    blocks = blocks.reshape(*shape, *blocks.shape[1:])
    blocks = blocks.transpose(*order, *range(len(axes), blocks.ndim))
    blocks = blocks.reshape(-1, *blocks.shape[len(axes) :])
    for k in order:
        blocks = lax.psum_scatter(blocks, axes[k], scatter_dimension=0, tiled=True)
    return blocks[0]


def in_blocks(array, dim, devices):
    shape = array.shape
    blocks = array.reshape(*shape[:dim], devices, shape[dim] // devices, *shape[dim + 1 :])
    return jnp.moveaxis(blocks, dim, 0)


def scatter_axes(array, axes, order, dim):
    devices = lax.axis_size(axes)
    return reduced_to_own(in_blocks(array, dim, devices), axes, order)


def joined_along(blocks, dim):
    shape = list(blocks.shape[1:])
    shape[dim] *= blocks.shape[0]
    return jnp.moveaxis(blocks, 0, dim).reshape(shape)


def sent_to_all(array, axis):
    copies = jnp.broadcast_to(array, (lax.axis_size(axis), *array.shape))
    return lax.all_to_all(copies, axis, split_axis=0, concat_axis=0, tiled=True)


def gather_directly(array, axis, dim):
    return joined_along(sent_to_all(array, axis), dim)


def of_everyone(array, axis):
    everything = sent_to_all(array, axis)
    return jnp.sum(everything, axis=0)


def neighbours(field):
    depth, flat = field.shape
    zero_plane = jnp.zeros((1, flat), field.dtype)
    total = jnp.concatenate([zero_plane, field[:-1]], 0) + jnp.concatenate(
        [field[1:], zero_plane], 0
    )
    zero_rows = jnp.zeros((depth, NX), field.dtype)
    total = (
        total
        + jnp.concatenate([zero_rows, field[:, :-NX]], 1)
        + jnp.concatenate([field[:, NX:], zero_rows], 1)
    )
    column = jnp.arange(flat) % NX
    zero_col = jnp.zeros((depth, 1), field.dtype)
    left = jnp.concatenate([zero_col, field[:, :-1]], 1) * (column > 0).astype(field.dtype)
    right = jnp.concatenate([field[:, 1:], zero_col], 1) * (column < NX - 1).astype(field.dtype)
    return total + left + right


def solve(psi, perturb, potential, energy):
    diag = 3.25 + potential - energy
    source = -perturb * psi
    answer = jnp.zeros_like(psi)
    for step in range(STEPS):
        weight = 1.0 / (1.0 + 0.8 * jnp.cos(jnp.pi * (2 * step + 1) / (2 * STEPS)))
        applied = diag * answer - 0.5 * neighbours(answer)
        answer = answer + weight * (source - applied) / diag
    return answer


def sine_basis(count):
    index = jnp.arange(count, dtype=jnp.float32) + 1.0
    return jnp.sqrt(2.0 / (count + 1)) * jnp.sin(
        jnp.pi * index[:, None] * index[None, :] / (count + 1)
    )


def eigen_of(position, count):
    return 2.0 - 2.0 * jnp.cos(jnp.pi * (position.astype(jnp.float32) + 1.0) / (count + 1))


def planes(field):
    high = lax.Precision.HIGHEST
    depth = field.shape[0]
    cube = field.reshape(depth, NY, NX)
    cube = jnp.einsum("zyx,cx->zyc", cube, sine_basis(NX), precision=high)
    cube = jnp.einsum("zyc,by->zbc", cube, sine_basis(NY), precision=high)
    return cube.reshape(depth, NY * NX)


def scale_columns(columns, start):
    high = lax.Precision.HIGHEST
    width = columns.shape[1]
    position = start + jnp.arange(width)
    denom = (
        eigen_of(jnp.arange(NZ), NZ)[:, None]
        + eigen_of(position // NX, NY)[None, :]
        + eigen_of(position % NX, NX)[None, :]
    )
    basis = sine_basis(NZ)
    spectral = jnp.dot(basis, columns, precision=high) * (jnp.sqrt(4.0 * jnp.pi) / jnp.sqrt(denom))
    return jnp.dot(basis, spectral, precision=high)


def coulomb_slab(slab):
    columns = lax.all_to_all(planes(slab), ORB, split_axis=1, concat_axis=0, tiled=True)
    scaled = scale_columns(columns, lax.axis_index(ORB) * columns.shape[1])
    back = lax.all_to_all(scaled, ORB, split_axis=0, concat_axis=1, tiled=True)
    return planes(back)


def factorize(partial_gram):
    lower = jnp.linalg.cholesky(partial_gram / (NZ * NY * NX))
    inverse = lax.linalg.triangular_solve(
        lower, jnp.eye(lower.shape[0], dtype=jnp.float32), left_side=True, lower=True
    )
    return (lower, inverse)


def body(orbitals, energies, trial_potential, local_potential):
    high = lax.Precision.HIGHEST
    depth = local_potential.shape[0]
    plane_cells = local_potential.shape[1]
    vector_slab = trial_potential.reshape(depth, plane_cells)
    perturb_full, potential_full = in_one_piece((vector_slab, local_potential), ORB, 0, 1)
    perturb = perturb_full.astype(jnp.float32)
    potential = potential_full.astype(jnp.float32)
    weight = 4.0 / (orbitals.shape[0] * lax.axis_size(ORB))
    psi = orbitals[0].astype(jnp.float32)
    partial_value = psi * solve(psi, perturb, potential, energies[0])
    partial_value = partial_value * weight
    slab = scatter_axes(partial_value, ORB, (1, 0), 0)
    slab = coulomb_slab(slab)
    mine = slab.reshape(1, depth, plane_cells)
    gathered = gather_directly(mine, "vec", 0)
    flat = gathered.reshape(gathered.shape[0], depth * plane_cells)
    partial_gram = jnp.dot(flat, flat.T, precision=high)
    lower, inverse = factorize(of_everyone(partial_gram, ORB))
    row = lax.dynamic_slice_in_dim(inverse, lax.axis_index("vec"), 1, 0)
    ortho = jnp.dot(row, flat, precision=high).reshape(1, depth, plane_cells)
    return (ortho, lower.T)


def solution(mesh):
    torus = Mesh(mesh.devices.reshape(16, 2, mesh.shape["vec"]), ("orb_0", "orb_1", "vec"))
    in_specs = (P(ORB, None, None), P(ORB), P("vec", ORB, None), P(ORB, None))
    out_specs = (P("vec", ORB, None), P())
    return jax.shard_map(body, mesh=torus, in_specs=in_specs, out_specs=out_specs, check_vma=False)
```

profile of v0, /device:TPU:1, one launch (start us, length us, event | category | flops | bytes accessed | tf_op | source)
XLA Modules:
  0.0 450.5 jit_solution(4015030020816501573)
XLA Ops:
  12.1 77.6 %all-gather.3.cloned.1.call-done = bf16[32,3,18432]{2,1,0:T(4,128)(2,1)} async-done(((bf16[1,3,18432]{2,1,0:T(4,128)(2,1)}), bf16[32,3,18432]{2,1,0:T(4,128)(2,1)}) %all-gather.3.cloned.1.call-update) | async-done | bytes 3538960 | tf_op jit(solution)/shard_map/all_gather | solution.py:20
  89.8 4.9 %reshape.125 = bf16[96,18432]{1,0:T(8,128)(2,1)S(1)} reshape(bf16[32,3,18432]{2,1,0:T(4,128)(2,1)} %all-gather.3.cloned.1.call-done) | data formatting | bytes 7077888
  94.6 3.2 multiply_divide_fusion
  98.5 4.2 fusion.85
  102.7 4.1 fusion.86
  106.8 7.2 %divide_add_fusion.1 = f32[96,9216]{1,0:T(8,128)S(1)} fusion(f32[96,9216]{1,0:T(8,128)S(1)} %multiply_divide_fusion, f32[96,9215]{1,0:T(8,128)} %get-tuple-element.31, f32[96,9215]{1,0:T(8,128)} %get-tuple-element.30, f32[96,9120]{1,0:T(8,128)} %get-tuple-element.29, f32[96,9120]{1,0:T(8,128)} %get-tuple-element.28, f32[95,9216]{1,0:T(8,128)S(1)} %get-tuple-element.27, ...), kind=kLoop, calls=%fused_computation.4 | loop fusion | flops 18579456 | bytes 33545476 | tf_op jit(solution)/shard_map/add | solution.py:90
  114.7 4.2 fusion.82
  118.8 4.1 fusion.83
  122.9 7.4 %divide_add_fusion = f32[96,9216]{1,0:T(8,128)S(1)} fusion(f32[96,9216]{1,0:T(8,128)S(1)} %divide_add_fusion.1, f32[96,9215]{1,0:T(8,128)} %get-tuple-element.25, f32[96,9215]{1,0:T(8,128)} %get-tuple-element.24, f32[96,9120]{1,0:T(8,128)} %get-tuple-element.23, f32[96,9120]{1,0:T(8,128)} %get-tuple-element.22, f32[95,9216]{1,0:T(8,128)S(1)} %get-tuple-element.21, ...), kind=kLoop, calls=%fused_computation.3 | loop fusion | flops 18579456 | bytes 33545476 | tf_op jit(solution)/shard_map/add | solution.py:90
  131.0 3.1 fusion.79
  134.1 4.3 fusion.80
  138.4 8.8 %fusion = f32[96,9216]{1,0:T(8,128)} fusion(f32[96,9216]{1,0:T(8,128)S(1)} %divide_add_fusion, f32[96,9215]{1,0:T(8,128)} %get-tuple-element.19, f32[96,9215]{1,0:T(8,128)} %get-tuple-element.18, f32[96,9120]{1,0:T(8,128)} %get-tuple-element.17, f32[96,9120]{1,0:T(8,128)S(1)} %get-tuple-element.16, f32[95,9216]{1,0:T(8,128)S(1)} %get-tuple-element.15, ...), kind=kLoop, calls=%fused_computation.2 | loop fusion | flops 20348928 | bytes 33545476 | tf_op jit(solution)/shard_map/mul | solution.py:154
  147.2 5.3 %reshape_reshape.9 = f32[16,2,3,9216]{3,2,1,0:T(4,128)} reshape(f32[96,9216]{1,0:T(8,128)} %fusion) | data formatting | bytes 7077888 | tf_op jit(solution)/shard_map/reshape;reshape | solution.py:25
  152.5 6.1 %copy.33 = f32[2,16,3,9216]{3,1,0,2:T(8,128)} copy(f32[2,16,3,9216]{3,2,0,1:T(4,128)} %bitcast.75) | data formatting | bytes 7077888 | tf_op jit(solution)/shard_map/transpose | solution.py:26
  158.7 19.3 %reduce-scatter.3.cloned.1.call-done = f32[16,3,9216]{2,0,1:T(8,128)} async-done(((f32[32,3,9216]{2,0,1:T(8,128)}), f32[16,3,9216]{2,0,1:T(8,128)}) %reduce-scatter.3.cloned.1.call-update) | async-done | bytes 1769488 | tf_op jit(solution)/shard_map/reduce_scatter | solution.py:29
  179.3 135.6 %all-reduce.25.cloned.1.call-done = f32[16,3,9216]{2,0,1:T(8,128)} async-done(((f32[16,3,9216]{2,0,1:T(8,128)}), f32[16,3,9216]{2,0,1:T(8,128)}) %all-reduce.25.cloned.1.call-update) | async-done | bytes 1769488
  319.1 17.7 %all-to-all-start = ((f32[3,32,288]{2,0,1:T(4,128)}), f32[3,32,288]{2,0,1:T(4,128)S(1)}, u32[]{:S(2)}, u32[]{:S(2)}) async-start(f32[3,32,288]{2,0,1:T(4,128)} %copy.34), calls=%async_computation.1 | async-start | bytes 393216 | tf_op jit(solution)/shard_map/all_to_all | solution.py:129
  336.9 18.7 %all-to-all-done = f32[3,32,288]{2,0,1:T(4,128)S(1)} async-done(((f32[3,32,288]{2,0,1:T(4,128)}), f32[3,32,288]{2,0,1:T(4,128)S(1)}, u32[]{:S(2)}, u32[]{:S(2)}) %all-to-all-start) | async-done | bytes 110624 | tf_op jit(solution)/shard_map/all_to_all | solution.py:129
  356.8 22.7 %all_to_all.45 = f32[32,3,288]{2,1,0:T(4,128)S(1)} all-to-all(f32[32,3,288]{2,1,0:T(4,128)S(1)} %all_to_all.36), channel_id=1, replica_groups=mesh['orb_0'=16,'orb_1'=2,'vec'=16] {'orb_0','orb_1'}, dimensions={0} | all-to-all | bytes 221184 | tf_op jit(solution)/shard_map/all_to_all | solution.py:131
  381.7 29.5 %all_to_all.46 = f32[16,1,3,9216]{3,1,2,0:T(1,128)S(1)} all-to-all(f32[16,1,3,9216]{3,1,2,0:T(1,128)S(1)} %broadcast_in_dim.8), channel_id=1, replica_groups=mesh['orb_0'=16,'orb_1'=2,'vec'=16] {'vec'}, dimensions={0} | all-to-all | bytes 3538944 | tf_op jit(solution)/shard_map/all_to_all | solution.py:52
  414.4 6.7 %all-to-all-start.3 = ((f32[32,1,256]{2,1,0:T(1,128)}), f32[32,1,256]{2,1,0:T(1,128)S(1)}, u32[]{:S(2)}, u32[]{:S(2)}) async-start(f32[32,1,256]{2,1,0:T(1,128)} %reshape.135), calls=%async_computation.4 | async-start | bytes 65536 | tf_op jit(solution)/shard_map/all_to_all | solution.py:52
  421.2 6.6 %reduce.7 = f32[16,3,9216]{2,1,0:T(4,128)} reduce(f32[16,1,3,9216]{3,1,2,0:T(1,128)S(1)} %all_to_all.46, f32[]{:T(128)} %constant.209), dimensions={1}, to_apply=%all_to_all.39.reduce_sub_computation | reduce | bytes 3538948 | tf_op jit(solution)/shard_map/all_to_all | solution.py:52
  427.8 5.4 %all-to-all-done.3 = f32[32,1,256]{2,1,0:T(1,128)S(1)} async-done(((f32[32,1,256]{2,1,0:T(1,128)}), f32[32,1,256]{2,1,0:T(1,128)S(1)}, u32[]{:S(2)}, u32[]{:S(2)}) %all-to-all-start.3) | async-done | bytes 32800 | tf_op jit(solution)/shard_map/all_to_all | solution.py:52
  439.0 3.5 fusion.1
  (66 shorter events, 25.5 us)
Async XLA Ops:
  7.2 82.6 %all-gather.3.cloned.1.call-start = ((), (), s32[]{:S(2)}) async-start(), calls=%async_computation.6 | async-start | bytes 4866048 | tf_op jit(solution)/shard_map/all_gather | solution.py:20
  8.9 169.1 %reduce-scatter.3.cloned.1.call-start = ((), (), s32[]{:S(2)}) async-start(), calls=%async_computation.5 | async-start | bytes 5308416 | tf_op jit(solution)/shard_map/reduce_scatter | solution.py:29
  102.7 4.1 copy-start
  102.7 4.1 copy-start.1
  102.7 4.1 copy-start.2
  158.7 156.3 %all-reduce.25.cloned.1.call-start = ((), (), s32[]{:S(2)}) async-start(), calls=%async_computation.7 | async-start | bytes 3538944
  319.1 36.5 %all-to-all-start = ((f32[3,32,288]{2,0,1:T(4,128)}), f32[3,32,288]{2,0,1:T(4,128)S(1)}, u32[]{:S(2)}, u32[]{:S(2)}) async-start(f32[3,32,288]{2,0,1:T(4,128)} %copy.34), calls=%async_computation.1 | async-start | bytes 393216 | tf_op jit(solution)/shard_map/all_to_all | solution.py:129
  414.4 18.8 %all-to-all-start.3 = ((f32[32,1,256]{2,1,0:T(1,128)}), f32[32,1,256]{2,1,0:T(1,128)S(1)}, u32[]{:S(2)}, u32[]{:S(2)}) async-start(f32[32,1,256]{2,1,0:T(1,128)} %reshape.135), calls=%async_computation.4 | async-start | bytes 65536 | tf_op jit(solution)/shard_map/all_to_all | solution.py:52
Sparse Core Ops, SparseCore 0:
  10.1 79.6 all-gather.2
  158.8 19.1 reduce-scatter.2
  180.3 134.5 all-reduce.24
where the time goes:
time: 451 us
  waiting for transfers between devices  257 us (57%)
  local copies, waits for them, and re-layouts  52.2 us (12%)
  blocking collectives  52.2 us (12%)
  other arithmetic  41.1 us (9%)
  starting transfers between devices  24.5 us (5%)
  between operations  14.6 us (3%)
  matrix products  9.13 us (2%)
    unnamed x4, waiting for transfers between devices  136 us
    all_gather x1, waiting for transfers between devices, in_one_piece(): lax.all_gather(both, axis, axis=dim, tiled=True)  77.6 us
    all_to_all x1, blocking collectives, sent_to_all(): return lax.all_to_all(copies, axis, split_axis=0, concat_axis=0, tiled=True)  29.5 us
    all_to_all x1, blocking collectives, coulomb_slab(): back = lax.all_to_all(scaled, ORB, split_axis=0, concat_axis=1, tiled=True)  22.7 us
    reduce_scatter x1, waiting for transfers between devices, reduced_to_own(): blocks = lax.psum_scatter(blocks, axes[k], scatter_dimension=0, tiled=True)  19.3 us
    all_to_all x1, waiting for transfers between devices, coulomb_slab(): lax.all_to_all(planes(slab), ORB, split_axis=1, concat_axis=0, tiled=True)  18.7 us
    all_to_all x1, starting transfers between devices, coulomb_slab(): lax.all_to_all(planes(slab), ORB, split_axis=1, concat_axis=0, tiled=True)  17.7 us
    add x2, other arithmetic, solve(): answer = answer + weight * (source - applied) / diag  14.6 us
  transfers between devices with their start and end apart: 5, of which 5 were waited for; matrix products, arithmetic and copies ran while one was open for 2% of the time, Pallas kernels for 0%

commit v1 on v0

v1 whole, which is shorter than its diff:
```python
import jax
import jax.numpy as jnp
import numpy as np
from jax import lax
from jax.experimental import pallas as pl
from jax.experimental.pallas import tpu as pltpu
from jax.sharding import PartitionSpec as P

NZ = 96
NY = 96
NX = 96
NYX = 9216
NORB = 32
NV = 16
F32 = jnp.float32
BF16 = jnp.bfloat16
HIGH = lax.Precision.HIGHEST
T4 = 8.0 / 0.8**4 - 8.0 / 0.8**2 + 1.0
Q0 = (T4 - 1.0) / T4
Q2 = (8.0 / 0.8**4) / T4
SCALE = 4.0 / NORB
ZORDER = (0, 2, 1, 3)


def sine(n):
    i = np.arange(n, dtype=np.float64) + 1.0
    return np.sqrt(2.0 / (n + 1)) * np.sin(np.pi * i[:, None] * i[None, :] / (n + 1))


def tables():
    s = sine(96)
    row_y = np.arange(96)
    y_of = 4 * (row_y % 24) + row_y // 24
    sx = np.zeros((128, 128))
    for g in range(32):
        for r in range(3):
            sx[:96, 4 * g + r] = s[:, 3 * g + r]
    sy = np.zeros((128, 128))
    for w in range(16):
        for i in range(6):
            sy[8 * w + i, :96] = s[6 * w + i, y_of]
    kz = np.kron(s, np.eye(4))
    pick = np.zeros((128, 128))
    same = np.zeros((128, 128))
    for a in range(128):
        pick[a, a // 8] = 1.0
        for b in range(128):
            same[a, b] = float(a % 8 == b % 8)
    small = np.stack([sx, sx.T, sy, sy.T, pick, pick.T, same])
    return small.astype(np.float32), kz.astype(np.float32)


def offset(x, q):
    base = 8 * (q % 2)
    if q < 2:
        return base + x
    return (base + 16 - x + jnp.where(x == 0, 4, 0)) % 16


def unpack(packed, lane):
    f0, f1, f2 = packed[:, :128], packed[:, 128:256], packed[:, 256:]
    y0 = jnp.where(lane < 96, f0, 0.0)
    y1 = jnp.where(lane < 32, pltpu.roll(f0, 32, 1), jnp.where(lane < 96, pltpu.roll(f1, 32, 1), 0.0))
    y2 = jnp.where(lane < 64, pltpu.roll(f1, 64, 1), jnp.where(lane < 96, pltpu.roll(f2, 64, 1), 0.0))
    y3 = jnp.where(lane < 96, pltpu.roll(f2, 96, 1), 0.0)
    return y0, y1, y2, y3


def pack(y, lane):
    r1, r2, r3 = pltpu.roll(y[1], 96, 1), pltpu.roll(y[2], 64, 1), pltpu.roll(y[3], 32, 1)
    return (
        jnp.where(lane < 96, y[0], r1),
        jnp.where(lane < 64, r1, r2),
        jnp.where(lane < 32, r2, r3),
    )


def kernel(
    psi_in, pert, pot, energy, small, kz_hbm, damp, out, factor,
    kz, psi_all, en_all, pv, vf, potf, cf, pdf, psif, gf, hf, mf, acc,
    pk, rc, rd, rx, x1, y1, u1, w1, u2, w2, x2, y2, t1, t2,
    zs, zr, es, er, xs, xr, hs, hr, ys, yr, cs, rs, rr,
    a1s, a1r, b1s, b1r, b2s, b2r, g1s, g1r, g2s, g2r, a2s, a2r, ks,
):
    o = lax.axis_index("orb")
    v = lax.axis_index("vec")
    z, c = o // 2, o % 2
    y, x = v // 4, v % 4
    mate = 2 * z + 1 - c

    def copy(src, dst, send, recv, orb, vec):
        return pltpu.make_async_remote_copy(
            src_ref=src, dst_ref=dst, send_sem=send, recv_sem=recv,
            device_id={"orb": orb, "vec": vec}, device_id_type=pl.DeviceIdType.MESH,
        )

    barrier = pltpu.get_barrier_semaphore()

    def greet(orb, vec):
        pl.semaphore_signal(
            barrier, inc=1, device_id={"orb": orb, "vec": vec}, device_id_type=pl.DeviceIdType.MESH
        )

    @pl.loop(1, 32)
    def _(d):
        greet((o + d) % 32, v)

    @pl.loop(1, 16)
    def _(d):
        greet(o, (v + d) % 16)
        greet(mate, (v + d) % 16)

    load_kz = pltpu.make_async_copy(kz_hbm, kz, ks)
    load_kz.start()
    own = 1 + c
    pv[own, x] = pert[...]
    pv[own, 4] = pot[...]
    for f in (gf, hf, mf):
        f[:, :, :8, :] = jnp.zeros((12, 4, 8, 128), F32)
        f[:, :, 32:, :] = jnp.zeros((12, 4, 8, 128), F32)
    acc[...] = jnp.zeros(acc.shape, F32)
    pl.semaphore_wait(barrier, 61)

    def z_copy(q):
        return copy(psi_in.at[q], psi_all.at[y, q], zs.at[q], zr.at[q], 2 * ((z + 16 - offset(x, q)) % 16) + c, v)

    def e_copy(q):
        return copy(energy, en_all.at[q], es.at[q], er.at[q], 2 * ((z + 16 - offset(x, q)) % 16) + c, v)

    def x_copy(d):
        return copy(pert, pv.at[own, x], xs.at[d - 1], xr.at[d - 1], o, 4 * y + (x + d) % 4)

    for d in (2, 1, 3):
        x_copy(d).start()

    @pl.when(x != 0)
    def _():
        z_copy(0).start()
        e_copy(0).start()

    @pl.when(x == 0)
    def _():
        psi_all[y, 0] = psi_in[0]
        en_all[0] = energy[...]

    for q in ZORDER[1:]:
        z_copy(q).start()
        e_copy(q).start()

    far = 3 - 3 * c
    h_mate = copy(pv.at[own], pv.at[own], hs.at[0], hr.at[0], mate, v)
    h_next = copy(pv.at[own], pv.at[far], hs.at[1], hr.at[1], 2 * ((z + 2 * c + 15) % 16) + c, v)
    h_pass = copy(pv.at[far], pv.at[far], hs.at[2], hr.at[2], mate, v)
    for d in (1, 2, 3):
        x_copy(d).wait()
    h_next.start()
    h_mate.start()

    def y_copy(q, d):
        return copy(psi_all.at[y, q], psi_all.at[y, q], ys.at[3 * q + d - 1], yr.at[3 * q + d - 1], o, 4 * ((y + d) % 4) + x)

    def spread(q):
        def arrived():
            z_copy(q).wait()
            e_copy(q).wait()

        if q == 0:
            pl.when(x != 0)(arrived)
        else:
            arrived()
        for d in (2, 1, 3):
            y_copy(q, d).start()

    lane = lax.broadcasted_iota(jnp.int32, (24, 128), 1)

    def solve(q):
        for d in (1, 2, 3):
            y_copy(q, d).wait()
        level = en_all[q, 0:1, :]

        @pl.loop(0, 12)
        def _(p):
            plane = 6 * z - 3 + p
            half = jnp.where((plane >= 0) & (plane < NZ), 0.5, 0.0)
            psi = unpack(psi_all[p // 3, q, p % 3].astype(F32), lane)
            for s in range(4):
                inverse = 1.0 / (3.25 + potf[p, s] - level)
                cf[p, s] = jnp.where(lane < 96, half * inverse, 0.0)
                pdf[p, s] = -psi[s] * inverse
                psif[p, s] = psi[s]

        def stencil(f, p):
            mid = [f[p, s, 8:32, :] for s in range(4)]
            total = []
            for s in range(4):
                up = mid[s - 1] if s > 0 else f[p, 3, 7:31, :]
                down = mid[s + 1] if s < 3 else f[p, 0, 9:33, :]
                n = (f[p - 1, s, 8:32, :] + f[p + 1, s, 8:32, :]) + (up + down)
                n = n + (pltpu.roll(mid[s], 1, 1) + pltpu.roll(mid[s], 127, 1))
                total.append(cf[p, s] * n)
            return mid, total

        @pl.loop(0, 4)
        def _(k):
            @pl.loop(0, 12)
            def _(p):
                for s in range(4):
                    gf[p, s, 8:32, :] = vf[k, p, s] * pdf[p, s]

            @pl.loop(1, 11)
            def _(p):
                mid, total = stencil(gf, p)
                for s in range(4):
                    hf[p, s, 8:32, :] = mid[s] + total[s]

            @pl.loop(2, 10)
            def _(p):
                _, total = stencil(hf, p)
                for s in range(4):
                    mf[p, s, 8:32, :] = total[s]

            @pl.loop(3, 9)
            def _(p):
                _, total = stencil(mf, p)
                for s in range(4):
                    answer = (SCALE * Q0) * hf[p, s, 8:32, :] + (SCALE * Q2) * total[s]
                    acc[k, p - 3, s] = acc[k, p - 3, s] + psif[p, s] * answer

    spread(0)
    spread(2)
    h_next.wait()
    h_pass.start()
    h_mate.wait()
    spread(1)
    h_pass.wait()

    @pl.loop(0, 12)
    def _(p):
        slab, t = p // 3, p % 3
        for k in range(4):
            field = unpack(pv[slab, k, t].astype(F32), lane)
            for s in range(4):
                vf[k, p, s] = field[s]
        field = unpack(pv[slab, 4, t].astype(F32), lane)
        for s in range(4):
            potf[p, s] = field[s]

    solve(0)
    spread(3)
    solve(2)
    solve(1)
    solve(3)

    @pl.loop(0, 4)
    def _(k):
        for p in range(6):
            f = pack([acc[k, p, s] for s in range(4)], lane)
            for t in range(3):
                pk[p // 3, k, p % 3, :, 128 * t : 128 * t + 128] = f[t]

    half_copy = copy(pk.at[1 - c], rc, cs.at[0], cs.at[1], mate, v)
    half_copy.start()
    half_copy.wait()
    for k in range(4):
        rd[k] = pk[c, k] + rc[k]

    def r_copy(d):
        to = (x + d) % 4
        return copy(rd.at[to], rx.at[d - 1], rs.at[d - 1], rr.at[d - 1], o, 4 * y + to)

    for d in (2, 1, 3):
        r_copy(d).start()
    for d in (1, 2, 3):
        r_copy(d).wait()

    def dot(a, b, dims=(((1,), (0,)), ((), ()))):
        return lax.dot_general(a, b, dims, precision=HIGH, preferred_element_type=F32)

    for p in range(3):
        total = (rd[x, p] + rx[0, p]) + (rx[1, p] + rx[2, p])
        plane = jnp.concatenate(unpack(total, lane), axis=0)
        plane = dot(small[2, :, :96], dot(plane, small[0]))
        x1[:, p] = plane.reshape(16, 8, 128)

    def layer_exchange(src, dst, send, recv):
        def one(d):
            to = (v + d) % 16
            return copy(src.at[to], dst.at[v], send.at[d], recv.at[d], o, to)

        @pl.loop(1, 16)
        def _(d):
            one(d).start()

        dst[v] = src[v]

        @pl.loop(1, 16)
        def _(d):
            one(d).wait()

    layer_exchange(x1, y1, a1s, a1r)

    def column_start(src, dst, send, recv):
        def one(d):
            to = (o + d) % 32
            return copy(src.at[to], dst.at[o], send.at[d], recv.at[d], to, v)

        @pl.loop(1, 32)
        def _(d):
            one(d).start()

        dst[o] = src[o]
        return one

    def column_wait(one):
        @pl.loop(1, 32)
        def _(d):
            one(d).wait()

    for p in range(3):
        flat = y1[:, p].reshape(128, 128)
        u1[:, p] = flat.T.reshape(32, 4, 128)
    first = column_start(u1, w1, b1s, b1r)
    column_wait(first)
    load_kz.wait()
    spectral = dot(kz[...], w1[...].reshape(384, 128)) * damp[...]
    u2[...] = dot(kz[...], spectral).reshape(32, 3, 4, 128)
    second = column_start(u2, w2, b2s, b2r)

    full = dot(spectral, spectral, (((0,), (0,)), ((), ()))) * small[6]
    gram = dot(small[5], dot(full, small[4]))[:16, :]
    slot = 2 * v + c
    t1[slot] = gram[:8] + pltpu.roll(gram[8:], 16, 1)

    def g1_copy(d, other):
        to = (v + d) % 16
        orb = mate if other else o
        return copy(t1.at[slot], t1.at[slot], g1s.at[2 * d + other], g1r.at[2 * d + other], orb, to)

    g1_copy(0, 1).start()

    @pl.loop(1, 16)
    def _(d):
        g1_copy(d, 0).start()
        g1_copy(d, 1).start()

    g1_copy(0, 1).wait()

    @pl.loop(1, 16)
    def _(d):
        g1_copy(d, 0).wait()
        g1_copy(d, 1).wait()

    t2[z] = jnp.sum(t1[...], axis=0)

    def g2_copy(d):
        return copy(t2.at[z], t2.at[z], g2s.at[d], g2r.at[d], 2 * ((z + d) % 16) + c, v)

    @pl.loop(1, 16)
    def _(d):
        g2_copy(d).start()

    @pl.loop(1, 16)
    def _(d):
        g2_copy(d).wait()

    folded = jnp.sum(t2[...], axis=0) * (1.0 / (NZ * NYX))
    row = lax.broadcasted_iota(jnp.int32, (16, 128), 0)
    col = lax.broadcasted_iota(jnp.int32, (16, 128), 1)
    work = jnp.concatenate([folded, pltpu.roll(folded, 112, 1)], axis=0)
    work = jnp.where(col < 16, work, jnp.where(col == row + 16, 1.0, 0.0))

    def eliminate(j, work):
        pivot_row = jnp.sum(jnp.where(row == j, work, 0.0), axis=0, keepdims=True)
        pivot_col = jnp.sum(jnp.where(col == j, work, 0.0), axis=1, keepdims=True)
        pivot = jnp.sum(jnp.where((row == j) & (col == j), work, 0.0), axis=(0, 1), keepdims=True)
        scaled = pivot_row * (1.0 / jnp.sqrt(pivot))
        reduced = work - (pivot_col * (1.0 / pivot)) * pivot_row
        return jnp.where(row == j, scaled, jnp.where(row > j, reduced, work))

    work = lax.fori_loop(0, 16, eliminate, work)
    factor[...] = jnp.where(col >= row, work, 0.0)[:, :16]
    right = pltpu.roll(work, 112, 1)
    right = jnp.where(col < 16, right, 0.0)
    right = jnp.concatenate([right, jnp.zeros((112, 128), F32)], axis=0)
    mix = dot(dot(small[4], right), small[5]) * small[6]

    column_wait(second)
    for p in range(3):
        flat = w2[:, p].reshape(128, 128)
        x2[:, p] = dot(mix, flat, (((1,), (1,)), ((), ()))).reshape(16, 8, 128)
    layer_exchange(x2, y2, a2s, a2r)
    for p in range(3):
        flat = y2[:, p].reshape(128, 128)
        plane = dot(dot(small[3, :96, :], flat), small[1])
        f = pack([plane[24 * s : 24 * s + 24] for s in range(4)], lane)
        for t in range(3):
            out[p, :, 128 * t : 128 * t + 128] = f[t]


def body(orbitals, energies, trial_potential, local_potential):
    o = lax.axis_index("orb")
    v = lax.axis_index("vec")
    z = o // 2
    y, x = v // 4, v % 4
    wanted = []
    for q in range(4):
        to = (z + 16 - offset(x, q)) % 16
        wanted.append(6 * to - 3 + 3 * y)
    at = jnp.concatenate([w + jnp.arange(3) for w in wanted])
    pickz = (at[:, None] == jnp.arange(NZ)[None, :]).astype(BF16)
    pieces = jnp.dot(pickz, orbitals[0], preferred_element_type=F32).astype(BF16)
    psi_in = pieces.reshape(4, 3, 24, 384)
    pert = trial_potential.reshape(3, 24, 384)
    pot = local_potential.reshape(3, 24, 384)
    energy = jnp.broadcast_to(energies.reshape(1, 1), (8, 128))
    i = jnp.arange(128)[None, :] % 8
    r = jnp.arange(384)[:, None]

    def eigen(position):
        return 2.0 - 2.0 * jnp.cos(jnp.pi * (position.astype(F32) + 1.0) / 97)

    denom = (eigen(r // 4) + eigen(6 * v + i)) + eigen(3 * o + r % 4)
    damp = jnp.where((i < 6) & (r % 4 < 3), jnp.sqrt(4.0 * jnp.pi) / jnp.sqrt(denom), 0.0)
    small, kz = tables()
    vmem = pl.BlockSpec(memory_space=pltpu.VMEM)
    dma = pltpu.SemaphoreType.DMA
    piece = (3, 24, 384)
    blocks = (12, 4, 24, 128)
    ortho, factor = pl.pallas_call(
        kernel,
        out_shape=(
            jax.ShapeDtypeStruct(piece, F32),
            jax.ShapeDtypeStruct((16, 16), F32),
        ),
        in_specs=[vmem] * 5 + [pl.BlockSpec(memory_space=pl.ANY), vmem],
        out_specs=(vmem, vmem),
        scratch_shapes=[
            pltpu.VMEM((384, 384), F32),
            pltpu.VMEM((4, 4) + piece, BF16),
            pltpu.VMEM((4, 8, 128), F32),
            pltpu.VMEM((4, 5) + piece, BF16),
            pltpu.VMEM((4,) + blocks, F32),
            pltpu.VMEM(blocks, F32),
            pltpu.VMEM(blocks, F32),
            pltpu.VMEM(blocks, F32),
            pltpu.VMEM(blocks, F32),
            pltpu.VMEM((12, 4, 40, 128), F32),
            pltpu.VMEM((12, 4, 40, 128), F32),
            pltpu.VMEM((12, 4, 40, 128), F32),
            pltpu.VMEM((4, 6, 4, 24, 128), F32),
            pltpu.VMEM((2, 4) + piece, F32),
            pltpu.VMEM((4,) + piece, F32),
            pltpu.VMEM((4,) + piece, F32),
            pltpu.VMEM((3,) + piece, F32),
            pltpu.VMEM((16, 3, 8, 128), F32),
            pltpu.VMEM((16, 3, 8, 128), F32),
            pltpu.VMEM((32, 3, 4, 128), F32),
            pltpu.VMEM((32, 3, 4, 128), F32),
            pltpu.VMEM((32, 3, 4, 128), F32),
            pltpu.VMEM((32, 3, 4, 128), F32),
            pltpu.VMEM((16, 3, 8, 128), F32),
            pltpu.VMEM((16, 3, 8, 128), F32),
            pltpu.VMEM((32, 8, 128), F32),
            pltpu.VMEM((16, 8, 128), F32),
            dma((4,)), dma((4,)), dma((4,)), dma((4,)), dma((3,)), dma((3,)), dma((3,)), dma((3,)),
            dma((12,)), dma((12,)), dma((2,)), dma((3,)), dma((3,)),
            dma((16,)), dma((16,)), dma((32,)), dma((32,)), dma((32,)), dma((32,)),
            dma((32,)), dma((32,)), dma((16,)), dma((16,)), dma((16,)), dma((16,)), dma(()),
        ],
        compiler_params=pltpu.CompilerParams(
            collective_id=0, has_side_effects=True, vmem_limit_bytes=48 << 20
        ),
    )(psi_in, pert, pot, energy, jnp.asarray(small), jnp.asarray(kz), damp)
    return ortho.reshape(1, 3, NYX), factor


def solution(mesh):
    in_specs = (P("orb", None, None), P("orb"), P("vec", "orb", None), P("orb", None))
    out_specs = (P("vec", "orb", None), P())
    return jax.shard_map(body, mesh=mesh, in_specs=in_specs, out_specs=out_specs, check_vma=False)
```

time: 451 us -> 144 us (0.32)
  waiting for transfers between devices: 257 us -> 0 us
  Pallas kernels: 0 us -> 138 us
  blocking collectives: 52.2 us -> 0 us
  local copies, waits for them, and re-layouts: 52.2 us -> 2.66 us
  other arithmetic: 41.1 us -> 0.42 us
  starting transfers between devices: 24.5 us -> 0 us
  between operations: 14.6 us -> 1.57 us
  matrix products: 9.13 us -> 0.39 us
    pallas_call x0 -> x1, Pallas kernels: none -> 138 us  [body(): pl.pallas_call(kernel, out_shape=(jax.ShapeDtypeStruct(piece, F32), jax.S...]
    unnamed x4 -> x0, waiting for transfers between devices: 136 us -> none
    all_gather x1 -> x0, waiting for transfers between devices: 77.6 us -> none  [in_one_piece(): lax.all_gather(both, axis, axis=dim, tiled=True)]
    all_to_all x2 -> x0, blocking collectives: 52.2 us -> none  [the longest x1 29.5 us: sent_to_all(): return lax.all_to_all(copies, axis, split_axis=0, concat_axis=0, tiled=True)]
    slice x9 -> x0, local copies, waits for them, and re-layouts: 25.8 us -> none  [the longest x3 12.5 us: neighbours(): field[:, :-1]]
    all_to_all x2 -> x0, starting transfers between devices: 24.4 us -> none  [the longest x1 17.7 us: coulomb_slab(): lax.all_to_all(planes(slab), ORB, split_axis=1, concat_axis=0, tiled=True)]
    all_to_all x2 -> x0, waiting for transfers between devices: 24.1 us -> none  [the longest x1 18.7 us: coulomb_slab(): lax.all_to_all(planes(slab), ORB, split_axis=1, concat_axis=0, tiled=True)]
    reduce_scatter x1 -> x0, waiting for transfers between devices: 19.3 us -> none  [reduced_to_own(): blocks = lax.psum_scatter(blocks, axes[k], scatter_dimension=0, tiled=True)]
  transfers between devices with their start and end apart: 5 -> 0, of which waited for: 5 -> 0; matrix products, arithmetic and copies ran while one was open for 2% -> 0% of each run, Pallas kernels for 0% -> 0%
where the time goes in v1:
time: 144 us; the launch traced here: 143 us
  Pallas kernels  138 us (96%)
  local copies, waits for them, and re-layouts  2.66 us (2%)
  between operations  1.57 us (1%)
    pallas_call x1, Pallas kernels, body(): pl.pallas_call(kernel, out_shape=(jax.ShapeDtypeStruct(piece, F32), jax.S...  138 us

profile of v1, /device:TPU:1, one launch (start us, length us, event | category | flops | bytes accessed | tf_op | source)
XLA Modules:
  0.0 143.5 jit_solution(13713795691565640489)
XLA Ops:
  0.6 0.0 copy-start
  0.7 0.0 copy-start.3
  0.7 0.0 copy-start.4
  0.8 0.1 pad_add_fusion
  0.9 1.2 copy-done
  2.1 0.0 copy-start.1
  2.1 0.0 copy-start.2
  2.1 0.4 convolution_convert_fusion
  2.6 0.1 fusion.8
  2.7 0.2 multiply_select_fusion.damp
  3.0 0.0 copy-done.3
  3.0 0.0 copy-done.4
  3.7 0.0 copy-done.1
  3.7 0.0 copy-done.2
  3.7 138.4 %shard_map.77 = (f32[3,24,384]{2,1,0:T(8,128)S(1)}, f32[16,16]{1,0:T(8,128)S(1)}) custom-call(bf16[4,3,24,384]{3,2,1,0:T(8,128)(2,1)S(1)} %bitcast.16, bf16[3,24,384]{2,1,0:T(8,128)(2,1)S(1)} %get-tuple-element.17.pert, bf16[3,24,384]{2,1,0:T(8,128)(2,1)S(1)} %get-tuple-element.16.pot, f32[8,128]{1,0:T(8,128)S(1)} %broadcast_in_dim.16.energy, ...), custom_call_target="tpu_custom_call" | custom-call | tf_op jit(solution)/shard_map/pallas_call | solution.py:429
  142.1 0.8 reshape.139
  142.9 0.6 copy.17
  (9 shorter events, 0.2 us)
Async XLA Ops:
  0.6 1.5 %copy-start = (bf16[1,96,9216]{2,1,0:T(8,128)(2,1)S(1)}, bf16[1,96,9216]{2,1,0:T(8,128)(2,1)}, u32[]{:S(2)}) copy-start(bf16[1,96,9216]{2,1,0:T(8,128)(2,1)} %param.6) | copy-start | bytes 5308420
  0.7 2.3 %copy-start.3 = (bf16[3,9216]{1,0:T(4,128)(2,1)S(1)}, bf16[3,9216]{1,0:T(4,128)(2,1)}, u32[]{:S(2)}) copy-start(bf16[3,9216]{1,0:T(4,128)(2,1)} %param.9) | copy-start | bytes 165892
  0.7 2.3 %copy-start.4 = (bf16[1,3,9216]{2,1,0:T(4,128)(2,1)S(1)}, bf16[1,3,9216]{2,1,0:T(4,128)(2,1)}, u32[]{:S(2)}) copy-start(bf16[1,3,9216]{2,1,0:T(4,128)(2,1)} %param.8) | copy-start | bytes 165892
  2.1 1.6 %copy-start.1 = (f32[384,384]{1,0:T(8,128)S(1)}, f32[384,384]{1,0:T(8,128)}, u32[]{:S(2)}) copy-start(f32[384,384]{1,0:T(8,128)} %constant.151.clone.kz_hbm) | copy-start | bytes 1769476
  2.1 1.6 %copy-start.2 = (f32[7,128,128]{2,1,0:T(8,128)S(1)}, f32[7,128,128]{2,1,0:T(8,128)}, u32[]{:S(2)}) copy-start(f32[7,128,128]{2,1,0:T(8,128)} %constant.150.clone.small) | copy-start | bytes 1376260

commit v2 on v1

--- a/solution.py
+++ b/solution.py
@@ -178,7 +178,7 @@
             y_copy(q, d).wait()
         level = en_all[q, 0:1, :]
 
-        @pl.loop(0, 12)
+        @pl.loop(0, 12, unroll=4)
         def _(p):
             plane = 6 * z - 3 + p
             half = jnp.where((plane >= 0) & (plane < NZ), 0.5, 0.0)
@@ -202,24 +202,24 @@
 
         @pl.loop(0, 4)
         def _(k):
-            @pl.loop(0, 12)
+            @pl.loop(0, 12, unroll=12)
             def _(p):
                 for s in range(4):
                     gf[p, s, 8:32, :] = vf[k, p, s] * pdf[p, s]
 
-            @pl.loop(1, 11)
+            @pl.loop(1, 11, unroll=10)
             def _(p):
                 mid, total = stencil(gf, p)
                 for s in range(4):
                     hf[p, s, 8:32, :] = mid[s] + total[s]
 
-            @pl.loop(2, 10)
+            @pl.loop(2, 10, unroll=8)
             def _(p):
                 _, total = stencil(hf, p)
                 for s in range(4):
                     mf[p, s, 8:32, :] = total[s]
 
-            @pl.loop(3, 9)
+            @pl.loop(3, 9, unroll=6)
             def _(p):
                 _, total = stencil(mf, p)
                 for s in range(4):

time: 144 us -> 113 us (0.78)
  Pallas kernels: 138 us -> 108 us
    pallas_call x1, Pallas kernels: 138 us -> 108 us  [body(): pl.pallas_call(kernel, out_shape=(jax.ShapeDtypeStruct(piece, F32), jax.S...]
where the time goes in v2:
time: 113 us
  Pallas kernels  108 us (96%)
  local copies, waits for them, and re-layouts  2.66 us (2%)
  between operations  1.57 us (1%)
    pallas_call x1, Pallas kernels, body(): pl.pallas_call(kernel, out_shape=(jax.ShapeDtypeStruct(piece, F32), jax.S...  108 us

profile of v2, /device:TPU:1, one launch (start us, length us, event | category | flops | bytes accessed | tf_op | source)
XLA Modules:
  0.0 113.1 jit_solution(1501580665110006264)
XLA Ops:
  0.6 0.0 copy-start
  0.7 0.0 copy-start.3
  0.7 0.0 copy-start.4
  0.8 0.1 pad_add_fusion
  0.9 1.2 %copy-done = bf16[1,96,9216]{2,1,0:T(8,128)(2,1)S(1)} copy-done((bf16[1,96,9216]{2,1,0:T(8,128)(2,1)S(1)}, bf16[1,96,9216]{2,1,0:T(8,128)(2,1)}, u32[]{:S(2)}) %copy-start) | copy-done | bytes 1769496
  2.1 0.0 copy-start.1
  2.1 0.0 copy-start.2
  2.1 0.4 convolution_convert_fusion
  2.6 0.1 fusion.8
  2.7 0.2 multiply_select_fusion.damp
  3.0 0.0 copy-done.3
  3.0 0.0 copy-done.4
  3.7 0.0 copy-done.1
  3.7 0.0 copy-done.2
  3.7 108.1 %shard_map.77 = (f32[3,24,384]{2,1,0:T(8,128)S(1)}, f32[16,16]{1,0:T(8,128)S(1)}) custom-call(bf16[4,3,24,384]{3,2,1,0:T(8,128)(2,1)S(1)} %bitcast.16, bf16[3,24,384]{2,1,0:T(8,128)(2,1)S(1)} %get-tuple-element.17.pert, bf16[3,24,384]{2,1,0:T(8,128)(2,1)S(1)} %get-tuple-element.16.pot, f32[8,128]{1,0:T(8,128)S(1)} %broadcast_in_dim.16.energy, ...), custom_call_target="tpu_custom_call" | custom-call | tf_op jit(solution)/shard_map/pallas_call | solution.py:429
  111.8 0.8 reshape.139
  112.5 0.6 copy.17
  (9 shorter events, 0.2 us)
Async XLA Ops:
  0.6 1.5 %copy-start = (bf16[1,96,9216]{2,1,0:T(8,128)(2,1)S(1)}, bf16[1,96,9216]{2,1,0:T(8,128)(2,1)}, u32[]{:S(2)}) copy-start(bf16[1,96,9216]{2,1,0:T(8,128)(2,1)} %param.6) | copy-start | bytes 5308420
  0.7 2.3 %copy-start.3 = (bf16[3,9216]{1,0:T(4,128)(2,1)S(1)}, bf16[3,9216]{1,0:T(4,128)(2,1)}, u32[]{:S(2)}) copy-start(bf16[3,9216]{1,0:T(4,128)(2,1)} %param.9) | copy-start | bytes 165892
  0.7 2.3 %copy-start.4 = (bf16[1,3,9216]{2,1,0:T(4,128)(2,1)S(1)}, bf16[1,3,9216]{2,1,0:T(4,128)(2,1)}, u32[]{:S(2)}) copy-start(bf16[1,3,9216]{2,1,0:T(4,128)(2,1)} %param.8) | copy-start | bytes 165892
  2.1 1.6 %copy-start.1 = (f32[384,384]{1,0:T(8,128)S(1)}, f32[384,384]{1,0:T(8,128)}, u32[]{:S(2)}) copy-start(f32[384,384]{1,0:T(8,128)} %constant.151.clone.kz_hbm) | copy-start | bytes 1769476
  2.1 1.6 %copy-start.2 = (f32[7,128,128]{2,1,0:T(8,128)S(1)}, f32[7,128,128]{2,1,0:T(8,128)}, u32[]{:S(2)}) copy-start(f32[7,128,128]{2,1,0:T(8,128)} %constant.150.clone.small) | copy-start | bytes 1376260

commit v3 on v2

--- a/solution.py
+++ b/solution.py
@@ -31,23 +31,26 @@
     s = sine(96)
     row_y = np.arange(96)
     y_of = 4 * (row_y % 24) + row_y // 24
-    sx = np.zeros((128, 128))
+    sx = np.zeros((2, 128, 128))
+    a, b, e = np.zeros((3, 96, 4, 32, 4))
     for g in range(32):
         for r in range(3):
-            sx[:96, 4 * g + r] = s[:, 3 * g + r]
+            sx[0, :96, 4 * g + r] = s[:, 3 * g + r]
+            sx[1, :96, 4 * g + (3, 2, 0)[r]] = s[:, 3 * g + r]
+            a[:, r, g, r] = s[:, 3 * g]
+            b[:, r, g, r] = s[:, 3 * g + 1]
+            e[:, 2, g, r] = s[:, 3 * g + 2]
+        a[:, 0, g, 3] = s[:, 3 * g + 2]
+        b[:, 1, g, 3] = s[:, 3 * g + 2]
     sy = np.zeros((128, 128))
     for w in range(16):
         for i in range(6):
             sy[8 * w + i, :96] = s[6 * w + i, y_of]
-    kz = np.kron(s, np.eye(4))
     pick = np.zeros((128, 128))
-    same = np.zeros((128, 128))
-    for a in range(128):
-        pick[a, a // 8] = 1.0
-        for b in range(128):
-            same[a, b] = float(a % 8 == b % 8)
-    small = np.stack([sx, sx.T, sy, sy.T, pick, pick.T, same])
-    return small.astype(np.float32), kz.astype(np.float32)
+    pick[np.arange(128), np.arange(128) // 8] = 1.0
+    small = np.stack([sx[0], sx[1], sy, sy.T, pick])
+    kz = np.concatenate([m.reshape(384, 128) for m in (a, b, e)], axis=1)
+    return small.astype(np.float32), np.stack([kz, kz.T]).astype(np.float32)
 
 
 def offset(x, q):
@@ -76,10 +79,10 @@
 
 
 def kernel(
-    psi_in, pert, pot, energy, small, kz_hbm, damp, out, factor,
-    kz, psi_all, en_all, pv, vf, potf, cf, pdf, psif, gf, hf, mf, acc,
+    psi_in, pert, pot, level_ref, small_hbm, kz_hbm, out, factor,
+    small, kz, damp, energy, psi_all, en_all, pv, vf, potf, cf, pdf, psif, gf, hf, mf, acc,
     pk, rc, rd, rx, x1, y1, u1, w1, u2, w2, x2, y2, t1, t2,
-    zs, zr, es, er, xs, xr, hs, hr, ys, yr, cs, rs, rr,
+    zs, zr, es, er, xs, xr, ns, nr, fs, fr, hs, hr, ys, yr, cs, cr, rs, rr,
     a1s, a1r, b1s, b1r, b2s, b2r, g1s, g1r, g2s, g2r, a2s, a2r, ks,
 ):
     o = lax.axis_index("orb")
@@ -110,8 +113,11 @@
         greet(o, (v + d) % 16)
         greet(mate, (v + d) % 16)
 
-    load_kz = pltpu.make_async_copy(kz_hbm, kz, ks)
+    load_small = pltpu.make_async_copy(small_hbm, small, ks.at[0])
+    load_kz = pltpu.make_async_copy(kz_hbm, kz, ks.at[1])
+    load_small.start()
     load_kz.start()
+    energy[...] = jnp.broadcast_to(level_ref[...], (8, 128))
     own = 1 + c
     pv[own, x] = pert[...]
     pv[own, 4] = pot[...]
@@ -119,6 +125,17 @@
         f[:, :, :8, :] = jnp.zeros((12, 4, 8, 128), F32)
         f[:, :, 32:, :] = jnp.zeros((12, 4, 8, 128), F32)
     acc[...] = jnp.zeros(acc.shape, F32)
+
+    def eigen(position):
+        return 2.0 - 2.0 * jnp.cos(jnp.pi * (position.astype(F32) + 1.0) / 97)
+
+    r8 = lax.broadcasted_iota(jnp.int32, (8, 128), 0)
+    i8 = lax.broadcasted_iota(jnp.int32, (8, 128), 1) % 8
+    plane_part = eigen(6 * v + i8) + eigen(3 * o + r8 % 4)
+    kept = (i8 < 6) & (r8 % 4 < 3)
+    for n in range(48):
+        denom = eigen(2 * n + r8 // 4) + plane_part
+        damp[8 * n : 8 * n + 8, :] = jnp.where(kept, jnp.sqrt(4.0 * jnp.pi) / jnp.sqrt(denom), 0.0)
     pl.semaphore_wait(barrier, 61)
 
     def z_copy(q):
@@ -130,6 +147,21 @@
     def x_copy(d):
         return copy(pert, pv.at[own, x], xs.at[d - 1], xr.at[d - 1], o, 4 * y + (x + d) % 4)
 
+    far = 3 - 3 * c
+    next_orb = 2 * ((z + 2 * c + 15) % 16) + c
+
+    def n_copy(k):
+        return copy((pert, pot)[k], pv.at[far, (x, 4)[k]], ns.at[k], nr.at[k], next_orb, v)
+
+    def f_copy(d):
+        return copy(pv.at[far, x], pv.at[far, x], fs.at[d - 1], fr.at[d - 1], o, 4 * y + (x + d) % 4)
+
+    def h_copy(k):
+        slab = (own, far)[k]
+        return copy(pv.at[slab], pv.at[slab], hs.at[k], hr.at[k], mate, v)
+
+    n_copy(0).start()
+    n_copy(1).start()
     for d in (2, 1, 3):
         x_copy(d).start()
 
@@ -146,15 +178,6 @@
     for q in ZORDER[1:]:
         z_copy(q).start()
         e_copy(q).start()
-
-    far = 3 - 3 * c
-    h_mate = copy(pv.at[own], pv.at[own], hs.at[0], hr.at[0], mate, v)
-    h_next = copy(pv.at[own], pv.at[far], hs.at[1], hr.at[1], 2 * ((z + 2 * c + 15) % 16) + c, v)
-    h_pass = copy(pv.at[far], pv.at[far], hs.at[2], hr.at[2], mate, v)
-    for d in (1, 2, 3):
-        x_copy(d).wait()
-    h_next.start()
-    h_mate.start()
 
     def y_copy(q, d):
         return copy(psi_all.at[y, q], psi_all.at[y, q], ys.at[3 * q + d - 1], yr.at[3 * q + d - 1], o, 4 * ((y + d) % 4) + x)
@@ -173,7 +196,33 @@
 
     lane = lax.broadcasted_iota(jnp.int32, (24, 128), 1)
 
-    def solve(q):
+    def vector(n):
+        return (x + jnp.where(n == 0, 2, jnp.where(n == 1, 1, jnp.where(n == 2, 3, 0)))) % 4
+
+    def half_copy(n):
+        return copy(pk.at[1 - c, vector(n)], rc.at[vector(n)], cs.at[n], cr.at[n], mate, v)
+
+    def r_copy(n):
+        return copy(rd.at[vector(n)], rx.at[n], rs.at[n], rr.at[n], o, 4 * y + vector(n))
+
+    def finish(n):
+        half_copy(n).wait()
+        rd[vector(n)] = pk[c, vector(n)] + rc[vector(n)]
+
+    def reduce(n):
+        k = vector(n)
+        for p in range(6):
+            f = pack([acc[k, p, s] for s in range(4)], lane)
+            for t in range(3):
+                pk[p // 3, k, p % 3, :, 128 * t : 128 * t + 128] = f[t]
+        half_copy(n).start()
+
+        @pl.when(n > 0)
+        def _():
+            finish(n - 1)
+            r_copy(n - 1).start()
+
+    def solve(q, after):
         for d in (1, 2, 3):
             y_copy(q, d).wait()
         level = en_all[q, 0:1, :]
@@ -201,7 +250,9 @@
             return mid, total
 
         @pl.loop(0, 4)
-        def _(k):
+        def _(n):
+            k = vector(n)
+
             @pl.loop(0, 12, unroll=12)
             def _(p):
                 for s in range(4):
@@ -226,60 +277,58 @@
                     answer = (SCALE * Q0) * hf[p, s, 8:32, :] + (SCALE * Q2) * total[s]
                     acc[k, p - 3, s] = acc[k, p - 3, s] + psif[p, s] * answer
 
+            if after is not None:
+                after(n)
+
+    def widen(slab):
+        @pl.loop(0, 3)
+        def _(n):
+            p = 3 * slab + n
+            for k in range(5):
+                field = unpack(pv[slab, k, n].astype(F32), lane)
+                for s in range(4):
+                    if k < 4:
+                        vf[k, p, s] = field[s]
+                    else:
+                        potf[p, s] = field[s]
+
+    n_copy(0).wait()
+    n_copy(1).wait()
+    for d in (2, 1, 3):
+        f_copy(d).start()
+    for d in (1, 2, 3):
+        x_copy(d).wait()
+    h_copy(0).start()
+    widen(own)
+    for d in (1, 2, 3):
+        f_copy(d).wait()
+    h_copy(1).start()
     spread(0)
+    widen(far)
     spread(2)
-    h_next.wait()
-    h_pass.start()
-    h_mate.wait()
+    h_copy(0).wait()
+    widen(2 - c)
+    h_copy(1).wait()
+    widen(3 * c)
     spread(1)
-    h_pass.wait()
-
-    @pl.loop(0, 12)
-    def _(p):
-        slab, t = p // 3, p % 3
-        for k in range(4):
-            field = unpack(pv[slab, k, t].astype(F32), lane)
-            for s in range(4):
-                vf[k, p, s] = field[s]
-        field = unpack(pv[slab, 4, t].astype(F32), lane)
-        for s in range(4):
-            potf[p, s] = field[s]
-
-    solve(0)
+    solve(0, None)
     spread(3)
-    solve(2)
-    solve(1)
-    solve(3)
-
-    @pl.loop(0, 4)
-    def _(k):
-        for p in range(6):
-            f = pack([acc[k, p, s] for s in range(4)], lane)
-            for t in range(3):
-                pk[p // 3, k, p % 3, :, 128 * t : 128 * t + 128] = f[t]
-
-    half_copy = copy(pk.at[1 - c], rc, cs.at[0], cs.at[1], mate, v)
-    half_copy.start()
-    half_copy.wait()
-    for k in range(4):
-        rd[k] = pk[c, k] + rc[k]
-
-    def r_copy(d):
-        to = (x + d) % 4
-        return copy(rd.at[to], rx.at[d - 1], rs.at[d - 1], rr.at[d - 1], o, 4 * y + to)
-
-    for d in (2, 1, 3):
-        r_copy(d).start()
-    for d in (1, 2, 3):
-        r_copy(d).wait()
+    solve(2, None)
+    solve(1, None)
+    solve(3, reduce)
+    finish(3)
+    for n in range(3):
+        r_copy(n).wait()
 
     def dot(a, b, dims=(((1,), (0,)), ((), ()))):
         return lax.dot_general(a, b, dims, precision=HIGH, preferred_element_type=F32)
 
+    load_small.wait()
+    load_kz.wait()
     for p in range(3):
         total = (rd[x, p] + rx[0, p]) + (rx[1, p] + rx[2, p])
         plane = jnp.concatenate(unpack(total, lane), axis=0)
-        plane = dot(small[2, :, :96], dot(plane, small[0]))
+        plane = dot(small[2, :, :96], dot(plane, small[p // 2]))
         x1[:, p] = plane.reshape(16, 8, 128)
 
     def layer_exchange(src, dst, send, recv):
@@ -316,25 +365,40 @@
         def _(d):
             one(d).wait()
 
-    for p in range(3):
-        flat = y1[:, p].reshape(128, 128)
-        u1[:, p] = flat.T.reshape(32, 4, 128)
+    big = (128, 128)
+    slot = lax.broadcasted_iota(jnp.int32, big, 0) % 4
+    lanes = lax.broadcasted_iota(jnp.int32, big, 1)
+    i = lanes % 8
+    across = (((1,), (1,)), ((), ()))
+    same = lax.broadcasted_iota(jnp.int32, big, 0) % 8 == i
+
+    def spare(f0, f1, f2):
+        moved = jnp.where(slot == 1, pltpu.roll(f1, 4, 1), jnp.where(slot == 2, pltpu.roll(f2, 2, 1), 0.0))
+        moved = jnp.where(slot == 0, pltpu.roll(f0, 6, 1), moved)
+        return jnp.where(i >= 6, moved, 0.0)
+
+    p0, p1, p2 = [y1[:, p].reshape(big).T for p in range(3)]
+    up1, up2 = pltpu.roll(p2, 1, 0), pltpu.roll(p2, 2, 0)
+    u1[:, 0] = (p0 + jnp.where(slot == 3, p2, 0.0) + spare(p2, up1, up2)).reshape(32, 4, 128)
+    u1[:, 1] = (p1 + jnp.where(slot == 3, up1, 0.0)).reshape(32, 4, 128)
     first = column_start(u1, w1, b1s, b1r)
     column_wait(first)
-    load_kz.wait()
-    spectral = dot(kz[...], w1[...].reshape(384, 128)) * damp[...]
-    u2[...] = dot(kz[...], spectral).reshape(32, 3, 4, 128)
-    second = column_start(u2, w2, b2s, b2r)
-
-    full = dot(spectral, spectral, (((0,), (0,)), ((), ()))) * small[6]
-    gram = dot(small[5], dot(full, small[4]))[:16, :]
-    slot = 2 * v + c
-    t1[slot] = gram[:8] + pltpu.roll(gram[8:], 16, 1)
+    half_a, half_b = w1[:, 0].reshape(big), w1[:, 1].reshape(big)
+    back = jnp.where((slot == 1) & (i >= 2) & (i < 4), pltpu.roll(half_a, 124, 1), 0.0)
+    back = jnp.where((slot == 2) & (i >= 4) & (i < 6), pltpu.roll(half_a, 126, 1), back)
+    back = jnp.where((slot == 0) & (i < 2), pltpu.roll(half_a, 122, 1), back)
+    spectral = dot(kz[0], jnp.concatenate([half_a, half_b, back], axis=0)) * damp[...]
+
+    full = dot(spectral, spectral, (((0,), (0,)), ((), ())))
+    full = jnp.sum(jnp.where(same, full, 0.0).reshape(16, 8, 128), axis=1)
+    gram = dot(full, small[4])
+    mine = 2 * v + c
+    t1[mine] = gram[:8] + pltpu.roll(gram[8:], 16, 1)
 
     def g1_copy(d, other):
         to = (v + d) % 16
         orb = mate if other else o
-        return copy(t1.at[slot], t1.at[slot], g1s.at[2 * d + other], g1r.at[2 * d + other], orb, to)
+        return copy(t1.at[mine], t1.at[mine], g1s.at[2 * d + other], g1r.at[2 * d + other], orb, to)
 
     g1_copy(0, 1).start()
 
@@ -343,6 +407,11 @@
         g1_copy(d, 0).start()
         g1_copy(d, 1).start()
 
+    columns = dot(kz[1], spectral)
+    extra = columns[256:]
+    u2[:, 0] = (columns[:128] + spare(extra, extra, extra)).reshape(32, 4, 128)
+    u2[:, 1] = columns[128:256].reshape(32, 4, 128)
+    second = column_start(u2, w2, b2s, b2r)
     g1_copy(0, 1).wait()
 
     @pl.loop(1, 16)
@@ -369,29 +438,30 @@
     work = jnp.concatenate([folded, pltpu.roll(folded, 112, 1)], axis=0)
     work = jnp.where(col < 16, work, jnp.where(col == row + 16, 1.0, 0.0))
 
-    def eliminate(j, work):
-        pivot_row = jnp.sum(jnp.where(row == j, work, 0.0), axis=0, keepdims=True)
-        pivot_col = jnp.sum(jnp.where(col == j, work, 0.0), axis=1, keepdims=True)
-        pivot = jnp.sum(jnp.where((row == j) & (col == j), work, 0.0), axis=(0, 1), keepdims=True)
-        scaled = pivot_row * (1.0 / jnp.sqrt(pivot))
-        reduced = work - (pivot_col * (1.0 / pivot)) * pivot_row
-        return jnp.where(row == j, scaled, jnp.where(row > j, reduced, work))
-
-    work = lax.fori_loop(0, 16, eliminate, work)
+    for j in range(15):
+        column = jnp.broadcast_to(work[:, j : j + 1], (16, 128))
+        ratio = work[j : j + 1, :] * (1.0 / column[j : j + 1, :])
+        work = work - jnp.where(row > j, column, 0.0) * ratio
+    pivots = jnp.sum(jnp.where(col == row, work, 0.0), axis=1, keepdims=True)
+    work = work * (1.0 / jnp.sqrt(pivots))
     factor[...] = jnp.where(col >= row, work, 0.0)[:, :16]
-    right = pltpu.roll(work, 112, 1)
-    right = jnp.where(col < 16, right, 0.0)
-    right = jnp.concatenate([right, jnp.zeros((112, 128), F32)], axis=0)
-    mix = dot(dot(small[4], right), small[5]) * small[6]
+    right = jnp.where(col < 16, pltpu.roll(work, 112, 1), 0.0)
+    right = dot(right, small[4], across)
+    mix = jnp.broadcast_to(right[:, None, :], (16, 8, 128)).reshape(big)
+    mix = jnp.where(same, mix, 0.0)
 
     column_wait(second)
-    for p in range(3):
-        flat = w2[:, p].reshape(128, 128)
-        x2[:, p] = dot(mix, flat, (((1,), (1,)), ((), ()))).reshape(16, 8, 128)
+    half_a, half_b = w2[:, 0].reshape(big), w2[:, 1].reshape(big)
+    back = jnp.where(i < 4, pltpu.roll(pltpu.roll(half_a, 127, 0), 124, 1), pltpu.roll(pltpu.roll(half_a, 126, 0), 126, 1))
+    back = jnp.where(i < 2, pltpu.roll(half_a, 122, 1), back)
+    third = jnp.where(slot == 3, half_a, jnp.where(slot == 2, pltpu.roll(half_b, 127, 0), 0.0))
+    third = jnp.where(slot == 0, jnp.where(i < 6, back, 0.0), third)
+    for p, plane in enumerate((half_a, half_b, third)):
+        x2[:, p] = dot(mix, plane, across).reshape(16, 8, 128)
     layer_exchange(x2, y2, a2s, a2r)
     for p in range(3):
         flat = y2[:, p].reshape(128, 128)
-        plane = dot(dot(small[3, :96, :], flat), small[1])
+        plane = dot(dot(small[3, :96, :], flat), small[p // 2], across)
         f = pack([plane[24 * s : 24 * s + 24] for s in range(4)], lane)
         for t in range(3):
             out[p, :, 128 * t : 128 * t + 128] = f[t]
@@ -412,15 +482,6 @@
     psi_in = pieces.reshape(4, 3, 24, 384)
     pert = trial_potential.reshape(3, 24, 384)
     pot = local_potential.reshape(3, 24, 384)
-    energy = jnp.broadcast_to(energies.reshape(1, 1), (8, 128))
-    i = jnp.arange(128)[None, :] % 8
-    r = jnp.arange(384)[:, None]
-
-    def eigen(position):
-        return 2.0 - 2.0 * jnp.cos(jnp.pi * (position.astype(F32) + 1.0) / 97)
-
-    denom = (eigen(r // 4) + eigen(6 * v + i)) + eigen(3 * o + r % 4)
-    damp = jnp.where((i < 6) & (r % 4 < 3), jnp.sqrt(4.0 * jnp.pi) / jnp.sqrt(denom), 0.0)
     small, kz = tables()
     vmem = pl.BlockSpec(memory_space=pltpu.VMEM)
     dma = pltpu.SemaphoreType.DMA
@@ -432,10 +493,13 @@
             jax.ShapeDtypeStruct(piece, F32),
             jax.ShapeDtypeStruct((16, 16), F32),
         ),
-        in_specs=[vmem] * 5 + [pl.BlockSpec(memory_space=pl.ANY), vmem],
+        in_specs=[vmem] * 4 + [pl.BlockSpec(memory_space=pltpu.HBM)] * 2,
         out_specs=(vmem, vmem),
         scratch_shapes=[
-            pltpu.VMEM((384, 384), F32),
+            pltpu.VMEM((5, 128, 128), F32),
+            pltpu.VMEM((2, 384, 384), F32),
+            pltpu.VMEM((384, 128), F32),
+            pltpu.VMEM((8, 128), F32),
             pltpu.VMEM((4, 4) + piece, BF16),
             pltpu.VMEM((4, 8, 128), F32),
             pltpu.VMEM((4, 5) + piece, BF16),
@@ -454,23 +518,23 @@
             pltpu.VMEM((3,) + piece, F32),
             pltpu.VMEM((16, 3, 8, 128), F32),
             pltpu.VMEM((16, 3, 8, 128), F32),
-            pltpu.VMEM((32, 3, 4, 128), F32),
-            pltpu.VMEM((32, 3, 4, 128), F32),
-            pltpu.VMEM((32, 3, 4, 128), F32),
-            pltpu.VMEM((32, 3, 4, 128), F32),
+            pltpu.VMEM((32, 2, 4, 128), F32),
+            pltpu.VMEM((32, 2, 4, 128), F32),
+            pltpu.VMEM((32, 2, 4, 128), F32),
+            pltpu.VMEM((32, 2, 4, 128), F32),
             pltpu.VMEM((16, 3, 8, 128), F32),
             pltpu.VMEM((16, 3, 8, 128), F32),
             pltpu.VMEM((32, 8, 128), F32),
             pltpu.VMEM((16, 8, 128), F32),
-            dma((4,)), dma((4,)), dma((4,)), dma((4,)), dma((3,)), dma((3,)), dma((3,)), dma((3,)),
-            dma((12,)), dma((12,)), dma((2,)), dma((3,)), dma((3,)),
+            dma((4,)), dma((4,)), dma((4,)), dma((4,)), dma((3,)), dma((3,)), dma((2,)), dma((2,)), dma((3,)), dma((3,)), dma((2,)), dma((2,)),
+            dma((12,)), dma((12,)), dma((4,)), dma((4,)), dma((3,)), dma((3,)),
             dma((16,)), dma((16,)), dma((32,)), dma((32,)), dma((32,)), dma((32,)),
-            dma((32,)), dma((32,)), dma((16,)), dma((16,)), dma((16,)), dma((16,)), dma(()),
+            dma((32,)), dma((32,)), dma((16,)), dma((16,)), dma((16,)), dma((16,)), dma((2,)),
         ],
         compiler_params=pltpu.CompilerParams(
             collective_id=0, has_side_effects=True, vmem_limit_bytes=48 << 20
         ),
-    )(psi_in, pert, pot, energy, jnp.asarray(small), jnp.asarray(kz), damp)
+    )(psi_in, pert, pot, energies.reshape(1, 1), jnp.asarray(small), jnp.asarray(kz))
     return ortho.reshape(1, 3, NYX), factor
 
 

time: 113 us -> 105 us (0.929)
  Pallas kernels: 108 us -> 101 us
    pallas_call x1, Pallas kernels: 108 us -> 101 us  [body(): pl.pallas_call(kernel, out_shape=(jax.ShapeDtypeStruct(piece, F32), jax.S...]
where the time goes in v3:
time: 105 us
  Pallas kernels  101 us (96%)
  local copies, waits for them, and re-layouts  2.64 us (3%)
  between operations  1.54 us (1%)
    pallas_call x1, Pallas kernels, body(): pl.pallas_call(kernel, out_shape=(jax.ShapeDtypeStruct(piece, F32), jax.S...  101 us

profile of v3, /device:TPU:1, one launch (start us, length us, event | category | flops | bytes accessed | tf_op | source)
XLA Modules:
  0.0 105.3 jit_solution(12359995879749155338)
XLA Ops:
  0.6 0.0 copy-start
  0.6 0.0 copy-start.4
  0.7 0.0 copy-start.3
  0.7 0.0 copy-start.1
  0.7 0.0 copy-start.2
  0.9 0.1 pad_add_fusion
  0.9 1.2 %copy-done = bf16[1,96,9216]{2,1,0:T(8,128)(2,1)S(1)} copy-done((bf16[1,96,9216]{2,1,0:T(8,128)(2,1)S(1)}, bf16[1,96,9216]{2,1,0:T(8,128)(2,1)}, u32[]{:S(2)}) %copy-start) | copy-done | bytes 1769496
  2.1 0.4 convolution_convert_fusion
  2.6 0.0 copy-done.4
  2.6 0.0 copy-done.3
  3.3 0.0 copy-done.1
  3.3 0.0 copy-done.2
  3.3 100.6 %shard_map.77 = (f32[3,24,384]{2,1,0:T(8,128)S(1)}, f32[16,16]{1,0:T(8,128)S(1)}) custom-call(bf16[4,3,24,384]{3,2,1,0:T(8,128)(2,1)S(1)} %bitcast.16, bf16[3,24,384]{2,1,0:T(8,128)(2,1)S(1)} %get-tuple-element.15.pert, bf16[3,24,384]{2,1,0:T(8,128)(2,1)S(1)} %get-tuple-element.14.pot, f32[1,1]{1,0:T(1,128)} %bitcast.15.level_ref, ...), custom_call_target="tpu_custom_call" | custom-call | tf_op jit(solution)/shard_map/pallas_call | solution.py:490
  103.9 0.8 reshape.25
  104.7 0.6 copy.17
  (5 shorter events, 0.1 us)
Async XLA Ops:
  0.6 1.5 %copy-start = (bf16[1,96,9216]{2,1,0:T(8,128)(2,1)S(1)}, bf16[1,96,9216]{2,1,0:T(8,128)(2,1)}, u32[]{:S(2)}) copy-start(bf16[1,96,9216]{2,1,0:T(8,128)(2,1)} %param.6) | copy-start | bytes 5308420
  0.6 1.9 %copy-start.4 = (bf16[1,3,9216]{2,1,0:T(4,128)(2,1)S(1)}, bf16[1,3,9216]{2,1,0:T(4,128)(2,1)}, u32[]{:S(2)}) copy-start(bf16[1,3,9216]{2,1,0:T(4,128)(2,1)} %param.8) | copy-start | bytes 165892
  0.7 1.9 %copy-start.3 = (bf16[3,9216]{1,0:T(4,128)(2,1)S(1)}, bf16[3,9216]{1,0:T(4,128)(2,1)}, u32[]{:S(2)}) copy-start(bf16[3,9216]{1,0:T(4,128)(2,1)} %param.9) | copy-start | bytes 165892
  0.7 2.6 %copy-start.1 = (f32[2,384,384]{2,1,0:T(8,128)S(1)}, f32[2,384,384]{2,1,0:T(8,128)}, u32[]{:S(2)}) copy-start(f32[2,384,384]{2,1,0:T(8,128)} %constant.92.clone.kz_hbm) | copy-start | bytes 3538948
  0.7 2.6 %copy-start.2 = (f32[5,128,128]{2,1,0:T(8,128)S(1)}, f32[5,128,128]{2,1,0:T(8,128)}, u32[]{:S(2)}) copy-start(f32[5,128,128]{2,1,0:T(8,128)} %constant.91.clone.small_hbm) | copy-start | bytes 983044

commit v4 on v3

--- a/solution.py
+++ b/solution.py
@@ -14,7 +14,6 @@
 NV = 16
 F32 = jnp.float32
 BF16 = jnp.bfloat16
-HIGH = lax.Precision.HIGHEST
 T4 = 8.0 / 0.8**4 - 8.0 / 0.8**2 + 1.0
 Q0 = (T4 - 1.0) / T4
 Q2 = (8.0 / 0.8**4) / T4
@@ -50,7 +49,9 @@
     pick[np.arange(128), np.arange(128) // 8] = 1.0
     small = np.stack([sx[0], sx[1], sy, sy.T, pick])
     kz = np.concatenate([m.reshape(384, 128) for m in (a, b, e)], axis=1)
-    return small.astype(np.float32), np.stack([kz, kz.T]).astype(np.float32)
+    kz_high = kz.astype(BF16)
+    kz_low = (kz - kz_high.astype(np.float64)).astype(BF16)
+    return small.astype(np.float32), np.stack([kz_high, kz_low, kz_high.T, kz_low.T])
 
 
 def offset(x, q):
@@ -222,7 +223,7 @@
             finish(n - 1)
             r_copy(n - 1).start()
 
-    def solve(q, after):
+    def prepare(q):
         for d in (1, 2, 3):
             y_copy(q, d).wait()
         level = en_all[q, 0:1, :]
@@ -238,6 +239,7 @@
                 pdf[p, s] = -psi[s] * inverse
                 psif[p, s] = psi[s]
 
+    def solve(q, low, high, after):
         def stencil(f, p):
             mid = [f[p, s, 8:32, :] for s in range(4)]
             total = []
@@ -249,7 +251,7 @@
                 total.append(cf[p, s] * n)
             return mid, total
 
-        @pl.loop(0, 4)
+        @pl.loop(low, high)
         def _(n):
             k = vector(n)
 
@@ -299,29 +301,44 @@
     for d in (1, 2, 3):
         x_copy(d).wait()
     h_copy(0).start()
+    spread(0)
+    spread(2)
     widen(own)
     for d in (1, 2, 3):
         f_copy(d).wait()
     h_copy(1).start()
-    spread(0)
     widen(far)
-    spread(2)
     h_copy(0).wait()
     widen(2 - c)
     h_copy(1).wait()
     widen(3 * c)
+    prepare(0)
+    solve(0, 0, 2, None)
     spread(1)
-    solve(0, None)
     spread(3)
-    solve(2, None)
-    solve(1, None)
-    solve(3, reduce)
+    solve(0, 2, 4, None)
+    prepare(2)
+    solve(2, 0, 4, None)
+    prepare(1)
+    solve(1, 0, 4, None)
+    prepare(3)
+    solve(3, 0, 4, reduce)
     finish(3)
     for n in range(3):
         r_copy(n).wait()
 
+    def halves(a):
+        high = a.astype(BF16)
+        return high, (a - high.astype(F32)).astype(BF16)
+
     def dot(a, b, dims=(((1,), (0,)), ((), ()))):
-        return lax.dot_general(a, b, dims, precision=HIGH, preferred_element_type=F32)
+        a_high, a_low = a if isinstance(a, tuple) else halves(a)
+        b_high, b_low = halves(b)
+
+        def product(l, r):
+            return lax.dot_general(l, r, dims, preferred_element_type=F32)
+
+        return product(a_high, b_high) + (product(a_high, b_low) + product(a_low, b_high))
 
     load_small.wait()
     load_kz.wait()
@@ -334,36 +351,28 @@
     def layer_exchange(src, dst, send, recv):
         def one(d):
             to = (v + d) % 16
-            return copy(src.at[to], dst.at[v], send.at[d], recv.at[d], o, to)
+            return copy(src.at[to], dst.at[v], send, recv, o, to)
 
         @pl.loop(1, 16)
         def _(d):
             one(d).start()
 
         dst[v] = src[v]
-
-        @pl.loop(1, 16)
-        def _(d):
-            one(d).wait()
+        copy(src.at[pl.ds(0, 15)], dst.at[pl.ds(0, 15)], send, recv, o, (v + 1) % 16).wait()
 
     layer_exchange(x1, y1, a1s, a1r)
 
     def column_start(src, dst, send, recv):
         def one(d):
             to = (o + d) % 32
-            return copy(src.at[to], dst.at[o], send.at[d], recv.at[d], to, v)
+            return copy(src.at[to], dst.at[o], send, recv, to, v)
 
         @pl.loop(1, 32)
         def _(d):
             one(d).start()
 
         dst[o] = src[o]
-        return one
-
-    def column_wait(one):
-        @pl.loop(1, 32)
-        def _(d):
-            one(d).wait()
+        return copy(src.at[pl.ds(0, 31)], dst.at[pl.ds(0, 31)], send, recv, (o + 1) % 32, v)
 
     big = (128, 128)
     slot = lax.broadcasted_iota(jnp.int32, big, 0) % 4
@@ -382,12 +391,12 @@
     u1[:, 0] = (p0 + jnp.where(slot == 3, p2, 0.0) + spare(p2, up1, up2)).reshape(32, 4, 128)
     u1[:, 1] = (p1 + jnp.where(slot == 3, up1, 0.0)).reshape(32, 4, 128)
     first = column_start(u1, w1, b1s, b1r)
-    column_wait(first)
+    first.wait()
     half_a, half_b = w1[:, 0].reshape(big), w1[:, 1].reshape(big)
     back = jnp.where((slot == 1) & (i >= 2) & (i < 4), pltpu.roll(half_a, 124, 1), 0.0)
     back = jnp.where((slot == 2) & (i >= 4) & (i < 6), pltpu.roll(half_a, 126, 1), back)
     back = jnp.where((slot == 0) & (i < 2), pltpu.roll(half_a, 122, 1), back)
-    spectral = dot(kz[0], jnp.concatenate([half_a, half_b, back], axis=0)) * damp[...]
+    spectral = dot((kz[0], kz[1]), jnp.concatenate([half_a, half_b, back], axis=0)) * damp[...]
 
     full = dot(spectral, spectral, (((0,), (0,)), ((), ())))
     full = jnp.sum(jnp.where(same, full, 0.0).reshape(16, 8, 128), axis=1)
@@ -398,7 +407,7 @@
     def g1_copy(d, other):
         to = (v + d) % 16
         orb = mate if other else o
-        return copy(t1.at[mine], t1.at[mine], g1s.at[2 * d + other], g1r.at[2 * d + other], orb, to)
+        return copy(t1.at[mine], t1.at[mine], g1s, g1r, orb, to)
 
     g1_copy(0, 1).start()
 
@@ -407,31 +416,22 @@
         g1_copy(d, 0).start()
         g1_copy(d, 1).start()
 
-    columns = dot(kz[1], spectral)
+    columns = dot((kz[2], kz[3]), spectral)
     extra = columns[256:]
     u2[:, 0] = (columns[:128] + spare(extra, extra, extra)).reshape(32, 4, 128)
     u2[:, 1] = columns[128:256].reshape(32, 4, 128)
     second = column_start(u2, w2, b2s, b2r)
-    g1_copy(0, 1).wait()
-
-    @pl.loop(1, 16)
-    def _(d):
-        g1_copy(d, 0).wait()
-        g1_copy(d, 1).wait()
-
+    copy(t1.at[pl.ds(0, 31)], t1.at[pl.ds(0, 31)], g1s, g1r, mate, v).wait()
     t2[z] = jnp.sum(t1[...], axis=0)
 
     def g2_copy(d):
-        return copy(t2.at[z], t2.at[z], g2s.at[d], g2r.at[d], 2 * ((z + d) % 16) + c, v)
+        return copy(t2.at[z], t2.at[z], g2s, g2r, 2 * ((z + d) % 16) + c, v)
 
     @pl.loop(1, 16)
     def _(d):
         g2_copy(d).start()
 
-    @pl.loop(1, 16)
-    def _(d):
-        g2_copy(d).wait()
-
+    copy(t2.at[pl.ds(0, 15)], t2.at[pl.ds(0, 15)], g2s, g2r, 2 * ((z + 1) % 16) + c, v).wait()
     folded = jnp.sum(t2[...], axis=0) * (1.0 / (NZ * NYX))
     row = lax.broadcasted_iota(jnp.int32, (16, 128), 0)
     col = lax.broadcasted_iota(jnp.int32, (16, 128), 1)
@@ -450,7 +450,7 @@
     mix = jnp.broadcast_to(right[:, None, :], (16, 8, 128)).reshape(big)
     mix = jnp.where(same, mix, 0.0)
 
-    column_wait(second)
+    second.wait()
     half_a, half_b = w2[:, 0].reshape(big), w2[:, 1].reshape(big)
     back = jnp.where(i < 4, pltpu.roll(pltpu.roll(half_a, 127, 0), 124, 1), pltpu.roll(pltpu.roll(half_a, 126, 0), 126, 1))
     back = jnp.where(i < 2, pltpu.roll(half_a, 122, 1), back)
@@ -497,7 +497,7 @@
         out_specs=(vmem, vmem),
         scratch_shapes=[
             pltpu.VMEM((5, 128, 128), F32),
-            pltpu.VMEM((2, 384, 384), F32),
+            pltpu.VMEM((4, 384, 384), BF16),
             pltpu.VMEM((384, 128), F32),
             pltpu.VMEM((8, 128), F32),
             pltpu.VMEM((4, 4) + piece, BF16),
@@ -528,8 +528,7 @@
             pltpu.VMEM((16, 8, 128), F32),
             dma((4,)), dma((4,)), dma((4,)), dma((4,)), dma((3,)), dma((3,)), dma((2,)), dma((2,)), dma((3,)), dma((3,)), dma((2,)), dma((2,)),
             dma((12,)), dma((12,)), dma((4,)), dma((4,)), dma((3,)), dma((3,)),
-            dma((16,)), dma((16,)), dma((32,)), dma((32,)), dma((32,)), dma((32,)),
-            dma((32,)), dma((32,)), dma((16,)), dma((16,)), dma((16,)), dma((16,)), dma((2,)),
+            *([dma(())] * 12), dma((2,)),
         ],
         compiler_params=pltpu.CompilerParams(
             collective_id=0, has_side_effects=True, vmem_limit_bytes=48 << 20

time: 105 us -> 97.2 us (0.926)
  Pallas kernels: 101 us -> 92.4 us
    pallas_call x1, Pallas kernels: 101 us -> 92.4 us  [body(): pl.pallas_call(kernel, out_shape=(jax.ShapeDtypeStruct(piece, F32), jax.S...]
where the time goes in v4:
time: 97.2 us; the launch traced here: 97 us
  Pallas kernels  92.4 us (95%)
  local copies, waits for them, and re-layouts  2.64 us (3%)
  between operations  1.54 us (2%)
    pallas_call x1, Pallas kernels, body(): pl.pallas_call(kernel, out_shape=(jax.ShapeDtypeStruct(piece, F32), jax.S...  92.4 us

profile of v4, /device:TPU:1, one launch (start us, length us, event | category | flops | bytes accessed | tf_op | source)
XLA Modules:
  0.0 97.0 jit_solution(12353222375737443588)
XLA Ops:
  0.6 0.0 copy-start
  0.6 0.0 copy-start.4
  0.7 0.0 copy-start.3
  0.7 0.0 copy-start.1
  0.7 0.0 copy-start.2
  0.9 0.1 pad_add_fusion
  0.9 1.2 %copy-done = bf16[1,96,9216]{2,1,0:T(8,128)(2,1)S(1)} copy-done((bf16[1,96,9216]{2,1,0:T(8,128)(2,1)S(1)}, bf16[1,96,9216]{2,1,0:T(8,128)(2,1)}, u32[]{:S(2)}) %copy-start) | copy-done | bytes 1769496
  2.1 0.4 convolution_convert_fusion
  2.6 0.0 copy-done.4
  2.6 0.0 copy-done.3
  3.3 0.0 copy-done.1
  3.3 0.0 copy-done.2
  3.3 92.4 %shard_map.77 = (f32[3,24,384]{2,1,0:T(8,128)S(1)}, f32[16,16]{1,0:T(8,128)S(1)}) custom-call(bf16[4,3,24,384]{3,2,1,0:T(8,128)(2,1)S(1)} %bitcast.16, bf16[3,24,384]{2,1,0:T(8,128)(2,1)S(1)} %get-tuple-element.15.pert, bf16[3,24,384]{2,1,0:T(8,128)(2,1)S(1)} %get-tuple-element.14.pot, f32[1,1]{1,0:T(1,128)} %bitcast.15.level_ref, ...), custom_call_target="tpu_custom_call" | custom-call | tf_op jit(solution)/shard_map/pallas_call | solution.py:490
  95.7 0.8 reshape.25
  96.4 0.6 copy.17
  (5 shorter events, 0.1 us)
Async XLA Ops:
  0.6 1.5 %copy-start = (bf16[1,96,9216]{2,1,0:T(8,128)(2,1)S(1)}, bf16[1,96,9216]{2,1,0:T(8,128)(2,1)}, u32[]{:S(2)}) copy-start(bf16[1,96,9216]{2,1,0:T(8,128)(2,1)} %param.6) | copy-start | bytes 5308420
  0.6 1.9 %copy-start.4 = (bf16[1,3,9216]{2,1,0:T(4,128)(2,1)S(1)}, bf16[1,3,9216]{2,1,0:T(4,128)(2,1)}, u32[]{:S(2)}) copy-start(bf16[1,3,9216]{2,1,0:T(4,128)(2,1)} %param.8) | copy-start | bytes 165892
  0.7 1.9 %copy-start.3 = (bf16[3,9216]{1,0:T(4,128)(2,1)S(1)}, bf16[3,9216]{1,0:T(4,128)(2,1)}, u32[]{:S(2)}) copy-start(bf16[3,9216]{1,0:T(4,128)(2,1)} %param.9) | copy-start | bytes 165892
  0.7 2.6 %copy-start.1 = (bf16[4,384,384]{2,1,0:T(8,128)(2,1)S(1)}, bf16[4,384,384]{2,1,0:T(8,128)(2,1)}, u32[]{:S(2)}) copy-start(bf16[4,384,384]{2,1,0:T(8,128)(2,1)} %constant.92.clone.kz_hbm) | copy-start | bytes 3538948
  0.7 2.6 %copy-start.2 = (f32[5,128,128]{2,1,0:T(8,128)S(1)}, f32[5,128,128]{2,1,0:T(8,128)}, u32[]{:S(2)}) copy-start(f32[5,128,128]{2,1,0:T(8,128)} %constant.91.clone.small_hbm) | copy-start | bytes 983044

commit v5 on v4

--- a/solution.py
+++ b/solution.py
@@ -81,7 +81,7 @@
 
 def kernel(
     psi_in, pert, pot, level_ref, small_hbm, kz_hbm, out, factor,
-    small, kz, damp, energy, psi_all, en_all, pv, vf, potf, cf, pdf, psif, gf, hf, mf, acc,
+    small, kz, tri, damp, energy, psi_all, en_all, pv, vf, potf, cf, pdf, psif, gf, hf, mf, acc,
     pk, rc, rd, rx, x1, y1, u1, w1, u2, w2, x2, y2, t1, t2,
     zs, zr, es, er, xs, xr, ns, nr, fs, fr, hs, hr, ys, yr, cs, cr, rs, rr,
     a1s, a1r, b1s, b1r, b2s, b2r, g1s, g1r, g2s, g2r, a2s, a2r, ks,
@@ -127,6 +127,12 @@
         f[:, :, 32:, :] = jnp.zeros((12, 4, 8, 128), F32)
     acc[...] = jnp.zeros(acc.shape, F32)
 
+    to = lax.broadcasted_iota(jnp.int32, (128, 128), 1)
+    gap = jnp.abs(to - lax.broadcasted_iota(jnp.int32, (128, 128), 0))
+    beside = jnp.where((gap == 1) & (to < 96), 1.0, 0.0).astype(BF16)
+    tri[:128, :] = beside
+    tri[128:, :] = beside
+
     def eigen(position):
         return 2.0 - 2.0 * jnp.cos(jnp.pi * (position.astype(F32) + 1.0) / 97)
 
@@ -243,11 +249,18 @@
         def stencil(f, p):
             mid = [f[p, s, 8:32, :] for s in range(4)]
             total = []
+            whole = jnp.concatenate(mid[2:], axis=0)
+            whole_high = whole.astype(BF16)
+            whole_low = (whole - whole_high.astype(F32)).astype(BF16)
+            beside = jnp.dot(jnp.concatenate([whole_high, whole_low], axis=1), tri[...], preferred_element_type=F32)
             for s in range(4):
                 up = mid[s - 1] if s > 0 else f[p, 3, 7:31, :]
                 down = mid[s + 1] if s < 3 else f[p, 0, 9:33, :]
                 n = (f[p - 1, s, 8:32, :] + f[p + 1, s, 8:32, :]) + (up + down)
-                n = n + (pltpu.roll(mid[s], 1, 1) + pltpu.roll(mid[s], 127, 1))
+                if s < 2:
+                    n = n + (pltpu.roll(mid[s], 1, 1) + pltpu.roll(mid[s], 127, 1))
+                else:
+                    n = n + beside[24 * s - 48 : 24 * s - 24]
                 total.append(cf[p, s] * n)
             return mid, total
 
@@ -498,6 +511,7 @@
         scratch_shapes=[
             pltpu.VMEM((5, 128, 128), F32),
             pltpu.VMEM((4, 384, 384), BF16),
+            pltpu.VMEM((256, 128), BF16),
             pltpu.VMEM((384, 128), F32),
             pltpu.VMEM((8, 128), F32),
             pltpu.VMEM((4, 4) + piece, BF16),

time: 97.2 us -> 97 us (level)
  no operation moved by 1% of the time
where the time goes in v5:
time: 97 us; the launch traced here: 96.9 us
  Pallas kernels  92.2 us (95%)
  local copies, waits for them, and re-layouts  2.64 us (3%)
  between operations  1.54 us (2%)
    pallas_call x1, Pallas kernels, body(): pl.pallas_call(kernel, out_shape=(jax.ShapeDtypeStruct(piece, F32), jax.S...  92.2 us

profile of v5, /device:TPU:1, one launch (start us, length us, event | category | flops | bytes accessed | tf_op | source)
XLA Modules:
  0.0 96.9 jit_solution(2732068647013902569)
XLA Ops:
  0.6 0.0 copy-start
  0.6 0.0 copy-start.4
  0.7 0.0 copy-start.3
  0.7 0.0 copy-start.1
  0.7 0.0 copy-start.2
  0.9 0.1 pad_add_fusion
  0.9 1.2 %copy-done = bf16[1,96,9216]{2,1,0:T(8,128)(2,1)S(1)} copy-done((bf16[1,96,9216]{2,1,0:T(8,128)(2,1)S(1)}, bf16[1,96,9216]{2,1,0:T(8,128)(2,1)}, u32[]{:S(2)}) %copy-start) | copy-done | bytes 1769496
  2.1 0.4 convolution_convert_fusion
  2.6 0.0 copy-done.4
  2.6 0.0 copy-done.3
  3.3 0.0 copy-done.1
  3.3 0.0 copy-done.2
  3.3 92.2 %shard_map.77 = (f32[3,24,384]{2,1,0:T(8,128)S(1)}, f32[16,16]{1,0:T(8,128)S(1)}) custom-call(bf16[4,3,24,384]{3,2,1,0:T(8,128)(2,1)S(1)} %bitcast.16, bf16[3,24,384]{2,1,0:T(8,128)(2,1)S(1)} %get-tuple-element.15.pert, bf16[3,24,384]{2,1,0:T(8,128)(2,1)S(1)} %get-tuple-element.14.pot, f32[1,1]{1,0:T(1,128)} %bitcast.15.level_ref, ...), custom_call_target="tpu_custom_call" | custom-call | tf_op jit(solution)/shard_map/pallas_call | solution.py:503
  95.5 0.8 reshape.25
  96.3 0.6 copy.17
  (5 shorter events, 0.1 us)
Async XLA Ops:
  0.6 1.5 %copy-start = (bf16[1,96,9216]{2,1,0:T(8,128)(2,1)S(1)}, bf16[1,96,9216]{2,1,0:T(8,128)(2,1)}, u32[]{:S(2)}) copy-start(bf16[1,96,9216]{2,1,0:T(8,128)(2,1)} %param.6) | copy-start | bytes 5308420
  0.6 1.9 %copy-start.4 = (bf16[1,3,9216]{2,1,0:T(4,128)(2,1)S(1)}, bf16[1,3,9216]{2,1,0:T(4,128)(2,1)}, u32[]{:S(2)}) copy-start(bf16[1,3,9216]{2,1,0:T(4,128)(2,1)} %param.8) | copy-start | bytes 165892
  0.7 1.9 %copy-start.3 = (bf16[3,9216]{1,0:T(4,128)(2,1)S(1)}, bf16[3,9216]{1,0:T(4,128)(2,1)}, u32[]{:S(2)}) copy-start(bf16[3,9216]{1,0:T(4,128)(2,1)} %param.9) | copy-start | bytes 165892
  0.7 2.6 %copy-start.1 = (bf16[4,384,384]{2,1,0:T(8,128)(2,1)S(1)}, bf16[4,384,384]{2,1,0:T(8,128)(2,1)}, u32[]{:S(2)}) copy-start(bf16[4,384,384]{2,1,0:T(8,128)(2,1)} %constant.92.clone.kz_hbm) | copy-start | bytes 3538948
  0.7 2.6 %copy-start.2 = (f32[5,128,128]{2,1,0:T(8,128)S(1)}, f32[5,128,128]{2,1,0:T(8,128)}, u32[]{:S(2)}) copy-start(f32[5,128,128]{2,1,0:T(8,128)} %constant.91.clone.small_hbm) | copy-start | bytes 983044

commit v6 on v5

--- a/solution.py
+++ b/solution.py
@@ -18,7 +18,6 @@
 Q0 = (T4 - 1.0) / T4
 Q2 = (8.0 / 0.8**4) / T4
 SCALE = 4.0 / NORB
-ZORDER = (0, 2, 1, 3)
 
 
 def sine(n):
@@ -83,7 +82,7 @@
     psi_in, pert, pot, level_ref, small_hbm, kz_hbm, out, factor,
     small, kz, tri, damp, energy, psi_all, en_all, pv, vf, potf, cf, pdf, psif, gf, hf, mf, acc,
     pk, rc, rd, rx, x1, y1, u1, w1, u2, w2, x2, y2, t1, t2,
-    zs, zr, es, er, xs, xr, ns, nr, fs, fr, hs, hr, ys, yr, cs, cr, rs, rr,
+    zs, zr, es, er, xs, xr, ns, nr, fs, fr, hs, hr, ys, yr, ps, qs, cs, cr, rs, rr,
     a1s, a1r, b1s, b1r, b2s, b2r, g1s, g1r, g2s, g2r, a2s, a2r, ks,
 ):
     o = lax.axis_index("orb")
@@ -148,6 +147,13 @@
     def z_copy(q):
         return copy(psi_in.at[q], psi_all.at[y, q], zs.at[q], zr.at[q], 2 * ((z + 16 - offset(x, q)) % 16) + c, v)
 
+    def plane_copy(q, n):
+        at = 6 * (q // 2) + 2 * n
+        return copy(
+            psi_in.at[q, n], psi_all.at[y, q, n], ps.at[at], ps.at[at + 1],
+            2 * ((z + 16 - offset(x, q)) % 16) + c, v,
+        )
+
     def e_copy(q):
         return copy(energy, en_all.at[q], es.at[q], er.at[q], 2 * ((z + 16 - offset(x, q)) % 16) + c, v)
 
@@ -182,12 +188,28 @@
         psi_all[y, 0] = psi_in[0]
         en_all[0] = energy[...]
 
-    for q in ZORDER[1:]:
-        z_copy(q).start()
+    z_copy(2).start()
+    e_copy(2).start()
+    for n in range(3):
+        for q in (1, 3):
+            plane_copy(q, n).start()
+    for q in (1, 3):
         e_copy(q).start()
 
     def y_copy(q, d):
         return copy(psi_all.at[y, q], psi_all.at[y, q], ys.at[3 * q + d - 1], yr.at[3 * q + d - 1], o, 4 * ((y + d) % 4) + x)
+
+    def part_copy(q, n, d):
+        at = 2 * (9 * (q // 2) + 3 * n + d - 1)
+        return copy(
+            psi_all.at[y, q, n], psi_all.at[y, q, n], qs.at[at], qs.at[at + 1], o, 4 * ((y + d) % 4) + x
+        )
+
+    def spread_plane(n):
+        for q in (1, 3):
+            plane_copy(q, n).wait()
+            for d in (2, 1, 3):
+                part_copy(q, n, d).start()
 
     def spread(q):
         def arrived():
@@ -231,7 +253,13 @@
 
     def prepare(q):
         for d in (1, 2, 3):
-            y_copy(q, d).wait()
+            if q % 2 == 0:
+                y_copy(q, d).wait()
+            else:
+                for n in range(3):
+                    part_copy(q, n, d).wait()
+        if q % 2 == 1:
+            e_copy(q).wait()
         level = en_all[q, 0:1, :]
 
         @pl.loop(0, 12, unroll=4)
@@ -324,11 +352,12 @@
     h_copy(0).wait()
     widen(2 - c)
     h_copy(1).wait()
+    spread_plane(0)
     widen(3 * c)
     prepare(0)
+    spread_plane(1)
     solve(0, 0, 2, None)
-    spread(1)
-    spread(3)
+    spread_plane(2)
     solve(0, 2, 4, None)
     prepare(2)
     solve(2, 0, 4, None)
@@ -541,7 +570,7 @@
             pltpu.VMEM((32, 8, 128), F32),
             pltpu.VMEM((16, 8, 128), F32),
             dma((4,)), dma((4,)), dma((4,)), dma((4,)), dma((3,)), dma((3,)), dma((2,)), dma((2,)), dma((3,)), dma((3,)), dma((2,)), dma((2,)),
-            dma((12,)), dma((12,)), dma((4,)), dma((4,)), dma((3,)), dma((3,)),
+            dma((12,)), dma((12,)), dma((12,)), dma((36,)), dma((4,)), dma((4,)), dma((3,)), dma((3,)),
             *([dma(())] * 12), dma((2,)),
         ],
         compiler_params=pltpu.CompilerParams(

time: 97 us -> 96.4 us (level)
  no operation moved by 1% of the time
where the time goes in v6:
time: 96.4 us; the launch traced here: 96.2 us
  Pallas kernels  91.6 us (95%)
  local copies, waits for them, and re-layouts  2.64 us (3%)
  between operations  1.54 us (2%)
    pallas_call x1, Pallas kernels, body(): pl.pallas_call(kernel, out_shape=(jax.ShapeDtypeStruct(piece, F32), jax.S...  91.6 us

profile of v6, /device:TPU:1, one launch (start us, length us, event | category | flops | bytes accessed | tf_op | source)
XLA Modules:
  0.0 96.2 jit_solution(1432689751531838752)
XLA Ops:
  0.6 0.0 copy-start
  0.6 0.0 copy-start.4
  0.7 0.0 copy-start.3
  0.7 0.0 copy-start.1
  0.7 0.0 copy-start.2
  0.9 0.1 pad_add_fusion
  0.9 1.2 %copy-done = bf16[1,96,9216]{2,1,0:T(8,128)(2,1)S(1)} copy-done((bf16[1,96,9216]{2,1,0:T(8,128)(2,1)S(1)}, bf16[1,96,9216]{2,1,0:T(8,128)(2,1)}, u32[]{:S(2)}) %copy-start) | copy-done | bytes 1769496
  2.1 0.4 convolution_convert_fusion
  2.6 0.0 copy-done.4
  2.6 0.0 copy-done.3
  3.3 0.0 copy-done.1
  3.3 0.0 copy-done.2
  3.3 91.6 %shard_map.77 = (f32[3,24,384]{2,1,0:T(8,128)S(1)}, f32[16,16]{1,0:T(8,128)S(1)}) custom-call(bf16[4,3,24,384]{3,2,1,0:T(8,128)(2,1)S(1)} %bitcast.16, bf16[3,24,384]{2,1,0:T(8,128)(2,1)S(1)} %get-tuple-element.15.pert, bf16[3,24,384]{2,1,0:T(8,128)(2,1)S(1)} %get-tuple-element.14.pot, f32[1,1]{1,0:T(1,128)} %bitcast.15.level_ref, ...), custom_call_target="tpu_custom_call" | custom-call | tf_op jit(solution)/shard_map/pallas_call | solution.py:532
  94.9 0.8 reshape.25
  95.7 0.6 copy.17
  (5 shorter events, 0.1 us)
Async XLA Ops:
  0.6 1.5 %copy-start = (bf16[1,96,9216]{2,1,0:T(8,128)(2,1)S(1)}, bf16[1,96,9216]{2,1,0:T(8,128)(2,1)}, u32[]{:S(2)}) copy-start(bf16[1,96,9216]{2,1,0:T(8,128)(2,1)} %param.6) | copy-start | bytes 5308420
  0.6 1.9 %copy-start.4 = (bf16[1,3,9216]{2,1,0:T(4,128)(2,1)S(1)}, bf16[1,3,9216]{2,1,0:T(4,128)(2,1)}, u32[]{:S(2)}) copy-start(bf16[1,3,9216]{2,1,0:T(4,128)(2,1)} %param.8) | copy-start | bytes 165892
  0.7 1.9 %copy-start.3 = (bf16[3,9216]{1,0:T(4,128)(2,1)S(1)}, bf16[3,9216]{1,0:T(4,128)(2,1)}, u32[]{:S(2)}) copy-start(bf16[3,9216]{1,0:T(4,128)(2,1)} %param.9) | copy-start | bytes 165892
  0.7 2.6 %copy-start.1 = (bf16[4,384,384]{2,1,0:T(8,128)(2,1)S(1)}, bf16[4,384,384]{2,1,0:T(8,128)(2,1)}, u32[]{:S(2)}) copy-start(bf16[4,384,384]{2,1,0:T(8,128)(2,1)} %constant.92.clone.kz_hbm) | copy-start | bytes 3538948
  0.7 2.6 %copy-start.2 = (f32[5,128,128]{2,1,0:T(8,128)S(1)}, f32[5,128,128]{2,1,0:T(8,128)}, u32[]{:S(2)}) copy-start(f32[5,128,128]{2,1,0:T(8,128)} %constant.91.clone.small_hbm) | copy-start | bytes 983044
